TPU v7x, 512 devices: a whole 4x8x8 slice. The times are simulated.
512 devices in a mesh: dp: 2 (over core), ctx: 32 (over z, x), tp: 8 (over y).
Axes of the slice: x: 4, y: 8, z: 8, core: 2. Of those that a mesh axis runs over, the one named last changes fastest.
Arguments:
- queries: bfloat16 [8192, 16384], P(('dp', 'ctx'), 'tp'), may hold values from -6 to 6
- keys: bfloat16 [8192, 1024], P(('dp', 'ctx'), 'tp'), may hold values from -6 to 6
- values: bfloat16 [8192, 1024], P(('dp', 'ctx'), 'tp'), may hold values from -6 to 6
- output_gradient: bfloat16 [8192, 16384], P(('dp', 'ctx'), 'tp'), may hold values from -6 to 6
- doc_lens: int32 [32], replicated, may hold values from 1 to 640, 8192 in all
Outputs:
- attended: bfloat16 [8192, 16384], P(('dp', 'ctx'), 'tp')
- query_grad: bfloat16 [8192, 16384], P(('dp', 'ctx'), 'tp')
- key_gradient_rows: bfloat16 [8192, 1024], P(('dp', 'ctx'), 'tp')
- value_gradient_rows: bfloat16 [8192, 1024], P(('dp', 'ctx'), 'tp')
Inputs may be any that keep to these rules, and one draw needn't show every extreme that they name: `doc_lens`: 32 lengths summing to 8192; the longest is exactly 640.
All inputs are finite; a program needn't handle non-finite values.
Results may differ from a plain program's by a relative error of at most 0.028.
Values may be sent and summed in bfloat16 or wider, within the bound.
No kernel may reach another device: no remote copies, remote signals or barrier semaphores. Data moves between devices by JAX's collectives and lax.ppermute only.
A program may use at most 64 MiB of HBM per device.

v0:
```python
import jax
import jax.numpy as jnp
from jax import lax
from jax.sharding import PartitionSpec as P

HEAD_SIZE = 128
BLOCK_TOKENS = 128
MOST_DEV = 5


NEG = -1e30


def passed_along(block, axis, distance):
    devices = range(lax.axis_size(axis))
    route = [(i - distance, i) for i in devices if i - distance in devices]
    return lax.ppermute(block, axis, route)


def doc_index(positions, ends):
    return jnp.sum((positions[:, None] >= ends[None, :]).astype(jnp.int32), axis=1)


def per_device(queries, keys, values, output_gradient, doc_lens):
    rows = queries.shape[0]
    scale = HEAD_SIZE ** (-0.5)
    carried = jnp.stack([keys, values])
    width = carried.shape[2]
    kv_local = width // HEAD_SIZE
    heads_here = queries.shape[1] // HEAD_SIZE
    per_group = heads_here // kv_local
    reach = MOST_DEV
    seq_index = lax.axis_index(("dp", "ctx"))
    pieces = []
    for offset in range(reach, 0, -1):
        pieces.append(passed_along(carried, ("dp", "ctx"), offset))
    window = jnp.concatenate(pieces + [carried], 1)
    span_rows = window.shape[1]
    base = (seq_index - reach) * rows
    ends = jnp.cumsum(doc_lens)
    key_pos = base + jnp.arange(span_rows, dtype=jnp.int32)
    key_doc = jnp.where(key_pos >= 0, doc_index(key_pos, ends), -1)
    query_pos = seq_index * rows + jnp.arange(rows, dtype=jnp.int32)
    query_doc = doc_index(query_pos, ends)
    key_span_rows = window[0].reshape(span_rows, kv_local, HEAD_SIZE)
    value_span_rows = window[1].reshape(span_rows, kv_local, HEAD_SIZE)
    query_all = queries.reshape(rows, kv_local, per_group, HEAD_SIZE)
    grad_all = output_gradient.reshape(rows, kv_local, per_group, HEAD_SIZE)
    blocks = rows // BLOCK_TOKENS
    key_gradients = jnp.zeros((span_rows, kv_local, HEAD_SIZE), jnp.float32)
    value_gradients = jnp.zeros((span_rows, kv_local, HEAD_SIZE), jnp.float32)
    query_block = query_all
    grad_block = grad_all
    qpos_block = query_pos
    qdoc_block = query_doc
    stop_tile = reach * blocks + 1

    def tile_data(tile, query_block=query_block, qpos_block=qpos_block, qdoc_block=qdoc_block):
        start_offset = tile * BLOCK_TOKENS
        key_tile = lax.dynamic_slice_in_dim(key_span_rows, start_offset, BLOCK_TOKENS, 0)
        value_tile = lax.dynamic_slice_in_dim(value_span_rows, start_offset, BLOCK_TOKENS, 0)
        kpos_tile = lax.dynamic_slice_in_dim(key_pos, start_offset, BLOCK_TOKENS, 0)
        kdoc_tile = lax.dynamic_slice_in_dim(key_doc, start_offset, BLOCK_TOKENS, 0)
        allowed = (qdoc_block[:, None] == kdoc_tile[None, :]) & (
            kpos_tile[None, :] <= qpos_block[:, None]
        )
        scores = (
            jnp.einsum("qhgd,khd->hgqk", query_block, key_tile, preferred_element_type=jnp.float32)
            * scale
        )
        return (key_tile, value_tile, allowed, scores)

    def statistics(tile, carry):
        running, total = carry
        unused_key, unused_value, allowed, scores = tile_data(tile)
        masked = jnp.where(allowed, scores, NEG)
        newest = jnp.maximum(running, jnp.max(masked, axis=-1))
        terms = jnp.where(allowed, jnp.exp(masked - newest[..., None]), 0.0)
        return (newest, total * jnp.exp(running - newest) + jnp.sum(terms, axis=-1))

    start_stats = (
        jnp.full((kv_local, per_group, BLOCK_TOKENS), NEG, jnp.float32),
        jnp.zeros((kv_local, per_group, BLOCK_TOKENS), jnp.float32),
    )
    running, total = lax.fori_loop(0, stop_tile, statistics, start_stats)
    log_total = running + jnp.log(total)

    def forward(tile, accum, log_total=log_total):
        unused_key, value_tile, allowed, scores = tile_data(tile)
        weights = jnp.where(allowed, jnp.exp(scores - log_total[..., None]), 0.0).astype(
            jnp.bfloat16
        )
        return accum + jnp.einsum(
            "hgqk,khd->qhgd", weights, value_tile, preferred_element_type=jnp.float32
        )

    accum = lax.fori_loop(
        0,
        stop_tile,
        forward,
        jnp.zeros((BLOCK_TOKENS, kv_local, per_group, HEAD_SIZE), jnp.float32),
    )
    attended_block = accum.astype(jnp.bfloat16)
    delta = jnp.einsum(
        "qhgd,qhgd->hgq", grad_block, attended_block, preferred_element_type=jnp.float32
    )

    def backward(
        tile,
        carry,
        log_total=log_total,
        delta=delta,
        grad_block=grad_block,
        query_block=query_block,
    ):
        query_accum, keys_accum, values_accum = carry
        key_tile, value_tile, allowed, scores = tile_data(tile)
        probs = jnp.where(allowed, jnp.exp(scores - log_total[..., None]), 0.0)
        weights = probs.astype(jnp.bfloat16)
        value_part = jnp.einsum(
            "hgqk,qhgd->khd", weights, grad_block, preferred_element_type=jnp.float32
        )
        spread = jnp.einsum(
            "qhgd,khd->hgqk", grad_block, value_tile, preferred_element_type=jnp.float32
        )
        score_grad = (probs * (spread - delta[..., None]) * scale).astype(jnp.bfloat16)
        query_accum = query_accum + jnp.einsum(
            "hgqk,khd->qhgd", score_grad, key_tile, preferred_element_type=jnp.float32
        )
        key_part = jnp.einsum(
            "hgqk,qhgd->khd", score_grad, query_block, preferred_element_type=jnp.float32
        )
        start_offset = tile * BLOCK_TOKENS
        keys_accum = lax.dynamic_update_slice_in_dim(
            keys_accum,
            lax.dynamic_slice_in_dim(keys_accum, start_offset, BLOCK_TOKENS, 0) + key_part,
            start_offset,
            0,
        )
        values_accum = lax.dynamic_update_slice_in_dim(
            values_accum,
            lax.dynamic_slice_in_dim(values_accum, start_offset, BLOCK_TOKENS, 0) + value_part,
            start_offset,
            0,
        )
        return (query_accum, keys_accum, values_accum)

    start_grads = (
        jnp.zeros((BLOCK_TOKENS, kv_local, per_group, HEAD_SIZE), jnp.float32),
        key_gradients,
        value_gradients,
    )
    query_accum, key_gradients, value_gradients = lax.fori_loop(0, stop_tile, backward, start_grads)
    outputs = attended_block.reshape(BLOCK_TOKENS, heads_here * HEAD_SIZE)
    query_grads = query_accum.astype(jnp.bfloat16).reshape(BLOCK_TOKENS, heads_here * HEAD_SIZE)
    grads = jnp.stack([key_gradients, value_gradients]).reshape(2, span_rows, width)
    parts = [
        grads[:, (reach - offset) * rows : (reach - offset + 1) * rows]
        for offset in range(reach + 1)
    ]
    summed = parts[0]
    for offset in range(1, reach + 1):
        summed = summed + passed_along(
            parts[offset].astype(jnp.bfloat16), ("dp", "ctx"), -offset
        ).astype(jnp.float32)
    return (outputs, query_grads, summed[0].astype(jnp.bfloat16), summed[1].astype(jnp.bfloat16))


def solution(mesh):
    return jax.shard_map(
        per_device,
        mesh=mesh,
        in_specs=(
            P(("dp", "ctx"), "tp"),
            P(("dp", "ctx"), "tp"),
            P(("dp", "ctx"), "tp"),
            P(("dp", "ctx"), "tp"),
            P(),
        ),
        out_specs=(
            P(("dp", "ctx"), "tp"),
            P(("dp", "ctx"), "tp"),
            P(("dp", "ctx"), "tp"),
            P(("dp", "ctx"), "tp"),
        ),
        check_vma=False,
    )
```

profile of v0, /device:TPU:1, one launch (start us, length us, event | category | flops | bytes accessed | tf_op | source)
XLA Modules:
  0.0 142.6 jit_solution(10340727753336216601)
XLA Ops:
  1.4 3.9 %collective-permute-start.4 = (bf16[2,128,128]{2,1,0:T(8,128)(2,1)S(1)}, bf16[2,128,128]{2,1,0:T(8,128)(2,1)S(1)}, u32[]{:S(2)}, u32[]{:S(2)}) collective-permute-start(bf16[2,128,128]{2,1,0:T(8,128)(2,1)S(1)} %pad_maximum_fusion), channel_id=1, source_target_pairs={{0,8},{8,16},{16,24},{24,32},{32,40},{40,48},{48,56},{56,64},{64,7... | collective-permute-start | bytes 196616 | tf_op jit(solution)/shard_map/ppermute | solution.py:17
  5.4 4.4 %collective-permute-start.3 = (bf16[2,128,128]{2,1,0:T(8,128)(2,1)S(1)}, bf16[2,128,128]{2,1,0:T(8,128)(2,1)S(1)}, u32[]{:S(2)}, u32[]{:S(2)}) collective-permute-start(bf16[2,128,128]{2,1,0:T(8,128)(2,1)S(1)} %pad_maximum_fusion), channel_id=1, source_target_pairs={{0,16},{8,24},{16,32},{24,40},{32,48},{40,56},{48,64},{56,72},{64,... | collective-permute-start | bytes 196616 | tf_op jit(solution)/shard_map/ppermute | solution.py:17
  9.7 4.9 %collective-permute-start.2 = (bf16[2,128,128]{2,1,0:T(8,128)(2,1)S(1)}, bf16[2,128,128]{2,1,0:T(8,128)(2,1)S(1)}, u32[]{:S(2)}, u32[]{:S(2)}) collective-permute-start(bf16[2,128,128]{2,1,0:T(8,128)(2,1)S(1)} %pad_maximum_fusion), channel_id=1, source_target_pairs={{0,24},{8,32},{16,40},{24,48},{32,56},{40,64},{48,72},{56,80},{64,... | collective-permute-start | bytes 196616 | tf_op jit(solution)/shard_map/ppermute | solution.py:17
  14.6 4.0 %collective-permute-start.1 = (bf16[2,128,128]{2,1,0:T(8,128)(2,1)S(1)}, bf16[2,128,128]{2,1,0:T(8,128)(2,1)S(1)}, u32[]{:S(2)}, u32[]{:S(2)}) collective-permute-start(bf16[2,128,128]{2,1,0:T(8,128)(2,1)S(1)} %pad_maximum_fusion), channel_id=1, source_target_pairs={{0,32},{8,40},{16,48},{24,56},{32,64},{40,72},{48,80},{56,88},{64,... | collective-permute-start | bytes 196616 | tf_op jit(solution)/shard_map/ppermute | solution.py:17
  18.6 4.0 %collective-permute-start = (bf16[2,128,128]{2,1,0:T(8,128)(2,1)S(1)}, bf16[2,128,128]{2,1,0:T(8,128)(2,1)S(1)}, u32[]{:S(2)}, u32[]{:S(2)}) collective-permute-start(bf16[2,128,128]{2,1,0:T(8,128)(2,1)S(1)} %pad_maximum_fusion), channel_id=1, source_target_pairs={{0,40},{8,48},{16,56},{24,64},{32,72},{40,80},{48,88},{56,96},{64,... | collective-permute-start | bytes 196616 | tf_op jit(solution)/shard_map/ppermute | solution.py:17
  25.6 2.0 %copy.33 = bf16[128,2048]{0,1:T(8,128)(2,1)} copy(bf16[128,2048]{1,0:T(8,128)(2,1)} %param.11) | data formatting | bytes 1048576 | tf_op args[0]
  27.6 1.4 copy.36
  30.9 1.3 copy.40
  33.8 23.4 %while.48 = (s32[]{:T(128)}, f32[1,16,128]{2,1,0:T(8,128)S(1)}, f32[1,16,128]{2,1,0:T(8,128)}, s32[128]{0:T(128)}, s32[768]{0:T(1024)}, /*index=5*/s32[768]{0:T(...) while((s32[]{:T(128)}, f32[1,16,128]{2,1,0:T(8,128)S(1)}, ...), condition=%wide.region_6.7_spmd.clone, body=%wide.region_3.6_spmd.clone.sunk | while | flops 68741256 | bytes 2880262 | solution.py:85
  57.2 1.3 log_add_fusion
  58.5 21.7 %while.49 = (s32[]{:T(128)}, f32[128,1,16,128]{0,3,2,1:T(8,128)S(1)}, bf16[768,1,128]{2,0,1:T(8,128)(2,1)S(1)}, s32[128]{0:T(128)}, s32[768]{0:T(1024)}, /*index...) while((s32[]{:T(128)}, ...), condition=%wide.region_8.9_spmd.clone, body=%wide.region_7.8_spmd.clone.sunk | while | flops 135839872 | bytes 2734288 | solution.py:97
  60.8 1.3 fusion.98
  64.4 1.3 fusion.98
  68.0 1.3 fusion.98
  71.6 1.3 fusion.98
  75.2 1.3 fusion.98
  78.8 1.3 fusion.98
  80.2 1.3 bitcast_convert_fusion
  81.5 1.7 %copy.50 = f32[16,128,128]{2,0,1:T(8,128)S(1)} copy(f32[16,128,128]{1,2,0:T(8,128)} %get-tuple-element.824) | data formatting | bytes 2097152
  83.3 2.0 %multiply_reduce_fusion = f32[16,128]{0,1:T(8,128)} fusion(f32[16,128,128]{2,0,1:T(8,128)S(1)} %copy.50, bf16[128,16,128]{2,1,0:T(8,128)(2,1)} %bitcast.243), kind=kLoop, calls=%fused_computation.75 | loop fusion | flops 784384 | bytes 1581056
  86.2 28.3 %while.50 = (s32[]{:T(128)}, f32[128,1,16,128]{0,3,2,1:T(8,128)S(1)}, f32[768,1,128]{2,0,1:T(8,128)S(1)}, f32[768,1,128]{2,0,1:T(8,128)S(1)}, bf16[768,1,128]{2,...) while((s32[]{:T(128)}, ...), condition=%wide.region_10.11_spmd.clone, body=%wide.region_9.10_spmd.clone.sunk | while | flops 338247808 | bytes 9327365 | solution.py:153
  93.2 1.1 fusion.109
  97.9 1.1 fusion.109
  102.7 1.1 fusion.109
  107.4 1.1 fusion.109
  112.1 1.1 fusion.109
  114.6 6.7 %collective-permute-start.5 = (bf16[2,128,128]{2,1,0:T(8,128)(2,1)S(1)}, bf16[2,128,128]{2,1,0:T(8,128)(2,1)S(1)}, u32[]{:S(2)}, u32[]{:S(2)}) collective-permute-start(bf16[2,128,128]{2,1,0:T(8,128)(2,1)S(1)} %get-tuple-element.828), channel_id=1, source_target_pairs={{8,0},{16,8},{24,16},{32,24},{40,32},{48,40},{56,48},{64,56},{72,6... | collective-permute-start | bytes 196616 | tf_op jit(solution)/shard_map/ppermute | solution.py:17
  121.3 2.3 %collective-permute-start.9 = (bf16[2,128,128]{2,1,0:T(8,128)(2,1)S(1)}, bf16[2,128,128]{2,1,0:T(8,128)(2,1)S(1)}, u32[]{:S(2)}, u32[]{:S(2)}) collective-permute-start(bf16[2,128,128]{2,1,0:T(8,128)(2,1)S(1)} %get-tuple-element.829), channel_id=1, source_target_pairs={{40,0},{48,8},{56,16},{64,24},{72,32},{80,40},{88,48},{96,56},{104... | collective-permute-start | bytes 196616 | tf_op jit(solution)/shard_map/ppermute | solution.py:17
  123.6 4.8 %collective-permute-start.8 = (bf16[2,128,128]{2,1,0:T(8,128)(2,1)S(1)}, bf16[2,128,128]{2,1,0:T(8,128)(2,1)S(1)}, u32[]{:S(2)}, u32[]{:S(2)}) collective-permute-start(bf16[2,128,128]{2,1,0:T(8,128)(2,1)S(1)} %get-tuple-element.830), channel_id=1, source_target_pairs={{32,0},{40,8},{48,16},{56,24},{64,32},{72,40},{80,48},{88,56},{96,... | collective-permute-start | bytes 196616 | tf_op jit(solution)/shard_map/ppermute | solution.py:17
  128.4 6.0 %collective-permute-start.7 = (bf16[2,128,128]{2,1,0:T(8,128)(2,1)S(1)}, bf16[2,128,128]{2,1,0:T(8,128)(2,1)S(1)}, u32[]{:S(2)}, u32[]{:S(2)}) collective-permute-start(bf16[2,128,128]{2,1,0:T(8,128)(2,1)S(1)} %get-tuple-element.831), channel_id=1, source_target_pairs={{24,0},{32,8},{40,16},{48,24},{56,32},{64,40},{72,48},{80,56},{88,... | collective-permute-start | bytes 196616 | tf_op jit(solution)/shard_map/ppermute | solution.py:17
  134.4 2.1 %collective-permute-start.6 = (bf16[2,128,128]{2,1,0:T(8,128)(2,1)S(1)}, bf16[2,128,128]{2,1,0:T(8,128)(2,1)S(1)}, u32[]{:S(2)}, u32[]{:S(2)}) collective-permute-start(bf16[2,128,128]{2,1,0:T(8,128)(2,1)S(1)} %get-tuple-element.832), channel_id=1, source_target_pairs={{16,0},{24,8},{32,16},{40,24},{48,32},{56,40},{64,48},{72,56},{80,... | collective-permute-start | bytes 196616 | tf_op jit(solution)/shard_map/ppermute | solution.py:17
  139.5 1.5 %collective-permute-done.6 = bf16[2,128,128]{2,1,0:T(8,128)(2,1)S(1)} collective-permute-done((bf16[2,128,128]{2,1,0:T(8,128)(2,1)S(1)}, bf16[2,128,128]{2,1,0:T(8,128)(2,1)S(1)}, u32[]{:S(2)}, u32[]{:S(2)}) %collective-permute-start.6) | collective-permute-done | bytes 65568 | tf_op jit(solution)/shard_map/ppermute | solution.py:17
  (203 shorter events, 71.9 us)
Async XLA Ops:
  1.4 31.6 %collective-permute-start.4 = (bf16[2,128,128]{2,1,0:T(8,128)(2,1)S(1)}, bf16[2,128,128]{2,1,0:T(8,128)(2,1)S(1)}, u32[]{:S(2)}, u32[]{:S(2)}) collective-permute-start(bf16[2,128,128]{2,1,0:T(8,128)(2,1)S(1)} %pad_maximum_fusion), channel_id=1, source_target_pairs={{0,8},{8,16},{16,24},{24,32},{32,40},{40,48},{48,56},{56,64},{64,7... | collective-permute-start | bytes 196616 | tf_op jit(solution)/shard_map/ppermute | solution.py:17
  5.4 27.6 %collective-permute-start.3 = (bf16[2,128,128]{2,1,0:T(8,128)(2,1)S(1)}, bf16[2,128,128]{2,1,0:T(8,128)(2,1)S(1)}, u32[]{:S(2)}, u32[]{:S(2)}) collective-permute-start(bf16[2,128,128]{2,1,0:T(8,128)(2,1)S(1)} %pad_maximum_fusion), channel_id=1, source_target_pairs={{0,16},{8,24},{16,32},{24,40},{32,48},{40,56},{48,64},{56,72},{64,... | collective-permute-start | bytes 196616 | tf_op jit(solution)/shard_map/ppermute | solution.py:17
  9.7 23.2 %collective-permute-start.2 = (bf16[2,128,128]{2,1,0:T(8,128)(2,1)S(1)}, bf16[2,128,128]{2,1,0:T(8,128)(2,1)S(1)}, u32[]{:S(2)}, u32[]{:S(2)}) collective-permute-start(bf16[2,128,128]{2,1,0:T(8,128)(2,1)S(1)} %pad_maximum_fusion), channel_id=1, source_target_pairs={{0,24},{8,32},{16,40},{24,48},{32,56},{40,64},{48,72},{56,80},{64,... | collective-permute-start | bytes 196616 | tf_op jit(solution)/shard_map/ppermute | solution.py:17
  14.6 18.3 %collective-permute-start.1 = (bf16[2,128,128]{2,1,0:T(8,128)(2,1)S(1)}, bf16[2,128,128]{2,1,0:T(8,128)(2,1)S(1)}, u32[]{:S(2)}, u32[]{:S(2)}) collective-permute-start(bf16[2,128,128]{2,1,0:T(8,128)(2,1)S(1)} %pad_maximum_fusion), channel_id=1, source_target_pairs={{0,32},{8,40},{16,48},{24,56},{32,64},{40,72},{48,80},{56,88},{64,... | collective-permute-start | bytes 196616 | tf_op jit(solution)/shard_map/ppermute | solution.py:17
  18.6 14.3 %collective-permute-start = (bf16[2,128,128]{2,1,0:T(8,128)(2,1)S(1)}, bf16[2,128,128]{2,1,0:T(8,128)(2,1)S(1)}, u32[]{:S(2)}, u32[]{:S(2)}) collective-permute-start(bf16[2,128,128]{2,1,0:T(8,128)(2,1)S(1)} %pad_maximum_fusion), channel_id=1, source_target_pairs={{0,40},{8,48},{16,56},{24,64},{32,72},{40,80},{48,88},{56,96},{64,... | collective-permute-start | bytes 196616 | tf_op jit(solution)/shard_map/ppermute | solution.py:17
  23.3 0.7 copy-start.6
  27.6 1.4 copy-start.1
  33.0 0.8 copy-start.4
  33.0 0.8 copy-start.5
  36.4 0.7 copy-start.2
  37.1 0.6 copy-start.3
  40.3 0.7 copy-start.2
  41.0 0.6 copy-start.3
  44.2 0.7 copy-start.2
  44.9 0.6 copy-start.3
  48.1 0.7 copy-start.2
  48.8 0.6 copy-start.3
  52.0 0.7 copy-start.2
  52.7 0.6 copy-start.3
  55.9 0.7 copy-start.2
  56.6 0.6 copy-start.3
  114.6 24.9 %collective-permute-start.5 = (bf16[2,128,128]{2,1,0:T(8,128)(2,1)S(1)}, bf16[2,128,128]{2,1,0:T(8,128)(2,1)S(1)}, u32[]{:S(2)}, u32[]{:S(2)}) collective-permute-start(bf16[2,128,128]{2,1,0:T(8,128)(2,1)S(1)} %get-tuple-element.828), channel_id=1, source_target_pairs={{8,0},{16,8},{24,16},{32,24},{40,32},{48,40},{56,48},{64,56},{72,6... | collective-permute-start | bytes 196616 | tf_op jit(solution)/shard_map/ppermute | solution.py:17
  121.3 18.2 %collective-permute-start.9 = (bf16[2,128,128]{2,1,0:T(8,128)(2,1)S(1)}, bf16[2,128,128]{2,1,0:T(8,128)(2,1)S(1)}, u32[]{:S(2)}, u32[]{:S(2)}) collective-permute-start(bf16[2,128,128]{2,1,0:T(8,128)(2,1)S(1)} %get-tuple-element.829), channel_id=1, source_target_pairs={{40,0},{48,8},{56,16},{64,24},{72,32},{80,40},{88,48},{96,56},{104... | collective-permute-start | bytes 196616 | tf_op jit(solution)/shard_map/ppermute | solution.py:17
  123.6 16.0 %collective-permute-start.8 = (bf16[2,128,128]{2,1,0:T(8,128)(2,1)S(1)}, bf16[2,128,128]{2,1,0:T(8,128)(2,1)S(1)}, u32[]{:S(2)}, u32[]{:S(2)}) collective-permute-start(bf16[2,128,128]{2,1,0:T(8,128)(2,1)S(1)} %get-tuple-element.830), channel_id=1, source_target_pairs={{32,0},{40,8},{48,16},{56,24},{64,32},{72,40},{80,48},{88,56},{96,... | collective-permute-start | bytes 196616 | tf_op jit(solution)/shard_map/ppermute | solution.py:17
  128.4 11.2 %collective-permute-start.7 = (bf16[2,128,128]{2,1,0:T(8,128)(2,1)S(1)}, bf16[2,128,128]{2,1,0:T(8,128)(2,1)S(1)}, u32[]{:S(2)}, u32[]{:S(2)}) collective-permute-start(bf16[2,128,128]{2,1,0:T(8,128)(2,1)S(1)} %get-tuple-element.831), channel_id=1, source_target_pairs={{24,0},{32,8},{40,16},{48,24},{56,32},{64,40},{72,48},{80,56},{88,... | collective-permute-start | bytes 196616 | tf_op jit(solution)/shard_map/ppermute | solution.py:17
  134.4 3.0 %copy-start = (bf16[128,1,16,128]{0,3,2,1:T(8,128)(2,1)S(1)}, bf16[128,1,16,128]{0,3,2,1:T(8,128)(2,1)}, u32[]{:S(2)}) copy-start(bf16[128,1,16,128]{0,3,2,1:T(8,128)(2,1)} %get-tuple-element.825) | copy-start | bytes 1572868
  134.4 6.6 %collective-permute-start.6 = (bf16[2,128,128]{2,1,0:T(8,128)(2,1)S(1)}, bf16[2,128,128]{2,1,0:T(8,128)(2,1)S(1)}, u32[]{:S(2)}, u32[]{:S(2)}) collective-permute-start(bf16[2,128,128]{2,1,0:T(8,128)(2,1)S(1)} %get-tuple-element.832), channel_id=1, source_target_pairs={{16,0},{24,8},{32,16},{40,24},{48,32},{56,40},{64,48},{72,56},{80,... | collective-permute-start | bytes 196616 | tf_op jit(solution)/shard_map/ppermute | solution.py:17
where the time goes:
time: 146 us; the launch traced here: 143 us
  local copies, waits for them, and re-layouts  47.4 us (32%)
  starting transfers between devices  43 us (29%)
  other arithmetic  24.5 us (17%)
  matrix products  24.4 us (17%)
  waiting for transfers between devices  1.53 us (1%)
    ppermute x10, starting transfers between devices, passed_along(): return lax.ppermute(block, axis, route)  43 us
    dynamic_slice x18, local copies, waits for them, and re-layouts, tile_data(): kpos_tile = lax.dynamic_slice_in_dim(key_pos, start_offset, BLOCK_TOKENS, 0)  13.7 us
    dynamic_slice x18, local copies, waits for them, and re-layouts, tile_data(): kdoc_tile = lax.dynamic_slice_in_dim(key_doc, start_offset, BLOCK_TOKENS, 0)  13.6 us
    and x18, other arithmetic, tile_data(): (qdoc_block[:, None] == kdoc_tile[None, :]) & (kpos_tile[None, :] <= qpos...  12.9 us
    unnamed x21, local copies, waits for them, and re-layouts  9.81 us
    dot_general x12, matrix products, tile_data(): jnp.einsum('qhgd,khd->hgqk', query_block, key_tile, preferred_element_typ...  8.23 us
    dot_general x6, matrix products, forward(): jnp.einsum('hgqk,khd->qhgd', weights, value_tile, preferred_element_type=...  8.01 us
    while x30, local copies, waits for them, and re-layouts  6.44 us
  transfers between devices with their start and end apart: 10, of which 1 were waited for; matrix products, arithmetic and copies ran while one was open for 9% of the time, Pallas kernels for 0%

commit v1 on v0

v1 whole, which is shorter than its diff:
```python
import jax
import jax.numpy as jnp
from jax import lax
from jax.experimental import pallas as pl
from jax.experimental.pallas import tpu as pltpu
from jax.sharding import PartitionSpec as P

HEAD = 128
TILE = 128
REACH = 5
SPAN = (REACH + 1) * TILE
SEQ_AXES = ("dp", "ctx")
SCALE = HEAD ** (-0.5)
LOG2E = 1.4426950408889634
NEG = -1e30

NT = (((1,), (1,)), ((), ()))
NN = (((1,), (0,)), ((), ()))


def dot(a, b, dims):
    return lax.dot_general(a, b, dims, preferred_element_type=jnp.float32)


def shifted(block, distance):
    devices = range(lax.axis_size(SEQ_AXES))
    route = [(i - distance, i) for i in devices if i - distance in devices]
    return lax.ppermute(block, SEQ_AXES, route)


def mask_bias(lens_ref, base, bias_ref):
    q_pos = base + REACH * TILE + lax.broadcasted_iota(jnp.int32, (8, TILE), 1)
    doc_start = jnp.zeros((8, TILE), jnp.int32)
    end = jnp.int32(0)
    for i in range(lens_ref.shape[0]):
        end = end + lens_ref[i]
        doc_start = jnp.where(q_pos >= end, jnp.maximum(doc_start, end), doc_start)
    q_pos, doc_start = q_pos[:1], doc_start[:1]
    for t in range(REACH + 1):
        k_pos = base + t * TILE + lax.broadcasted_iota(jnp.int32, (TILE, TILE), 0)
        seen = (k_pos >= doc_start) & (k_pos <= q_pos)
        bias_ref[pl.ds(t * TILE, TILE), :] = jnp.where(seen, 0.0, NEG)


def kernel(
    lens_ref, index_ref, q_ref, do_ref, far_ref, mid_ref, near_ref,
    o_ref, dq_ref, grads_ref,
    bias_ref, k_ref, v_ref, kt_ref, vt_ref, dk_ref, dv_ref,
):
    base = (index_ref[0] - REACH) * TILE
    mask_bias(lens_ref, base, bias_ref)
    for t, ref in enumerate((far_ref, mid_ref, near_ref)):
        rows = pl.ds(t * 2 * TILE, 2 * TILE)
        k = ref[:, :HEAD]
        v = ref[:, HEAD:]
        k_ref[rows, :] = k
        v_ref[rows, :] = v
        kt_ref[:, rows] = k.T
        vt_ref[:, rows] = v.T
    dk_ref[...] = jnp.zeros_like(dk_ref)
    dv_ref[...] = jnp.zeros_like(dv_ref)

    def pair(step, carry):
        at = pl.multiple_of(step * 2 * HEAD, 2 * HEAD)
        first, second = pl.ds(at, HEAD), pl.ds(pl.multiple_of(at + HEAD, HEAD), HEAD)
        q = jnp.concatenate([q_ref[:, first], q_ref[:, second]], 0)
        do = jnp.concatenate([do_ref[:, first], do_ref[:, second]], 0)
        bias = bias_ref[...]
        s = dot(k_ref[...], q, NT) * (SCALE * LOG2E) + jnp.concatenate([bias, bias], 1)
        m = jnp.max(s, axis=0, keepdims=True)
        p = jnp.exp2(s - m)
        p = p * (1.0 / jnp.sum(p, axis=0, keepdims=True))
        w = p.astype(jnp.bfloat16)
        dp = dot(v_ref[...], do, NT)
        delta = jnp.sum(p * dp, axis=0, keepdims=True)
        ds = (p * (dp - delta)).astype(jnp.bfloat16)
        dv_ref[...] += dot(w, do, NN)
        dk_ref[...] += dot(ds, q, NN)
        o = dot(vt_ref[...], w, NN).astype(jnp.bfloat16)
        dq = (dot(kt_ref[...], ds, NN) * SCALE).astype(jnp.bfloat16)
        o_ref[:, first] = o[:, :TILE].T
        o_ref[:, second] = o[:, TILE:].T
        dq_ref[:, first] = dq[:, :TILE].T
        dq_ref[:, second] = dq[:, TILE:].T
        return carry

    lax.fori_loop(0, q_ref.shape[1] // (2 * HEAD), pair, 0)
    grads_ref[:, :HEAD] = (dk_ref[...] * SCALE).astype(jnp.bfloat16)
    grads_ref[:, HEAD:] = dv_ref[...].astype(jnp.bfloat16)


def attention(lens, index, q, do, far, mid, near):
    vmem = pl.BlockSpec(memory_space=pltpu.VMEM)
    smem = pl.BlockSpec(memory_space=pltpu.SMEM)
    return pl.pallas_call(
        kernel,
        out_shape=(
            jax.ShapeDtypeStruct(q.shape, jnp.bfloat16),
            jax.ShapeDtypeStruct(q.shape, jnp.bfloat16),
            jax.ShapeDtypeStruct((SPAN, 2 * HEAD), jnp.bfloat16),
        ),
        in_specs=[smem, smem] + [vmem] * 5,
        out_specs=(vmem,) * 3,
        scratch_shapes=[
            pltpu.VMEM((SPAN, TILE), jnp.float32),
            pltpu.VMEM((SPAN, HEAD), jnp.bfloat16),
            pltpu.VMEM((SPAN, HEAD), jnp.bfloat16),
            pltpu.VMEM((HEAD, SPAN), jnp.bfloat16),
            pltpu.VMEM((HEAD, SPAN), jnp.bfloat16),
            pltpu.VMEM((SPAN, HEAD), jnp.float32),
            pltpu.VMEM((SPAN, HEAD), jnp.float32),
        ],
        compiler_params=pltpu.CompilerParams(vmem_limit_bytes=32 << 20),
        cost_estimate=pl.CostEstimate(
            flops=12 * SPAN * HEAD * q.shape[0] * (q.shape[1] // HEAD),
            transcendentals=SPAN * q.shape[0] * (q.shape[1] // HEAD),
            bytes_accessed=4 * q.size * 2 + 4 * SPAN * 2 * HEAD,
        ),
    )(lens, index, q, do, far, mid, near)


def per_device(queries, keys, values, output_gradient, doc_lens):
    index = lax.axis_index(SEQ_AXES).astype(jnp.int32)
    own = jnp.concatenate([keys, values], 1)
    before = shifted(own, 1)
    near = jnp.concatenate([before, own], 0)
    far = shifted(near, 4)
    mid = shifted(near, 2)
    attended, query_grad, grads = attention(
        doc_lens, index.reshape(1), queries, output_gradient, far, mid, near
    )
    from_far = shifted(grads[: 2 * TILE], -4).astype(jnp.float32)
    from_mid = shifted(grads[2 * TILE : 4 * TILE], -2).astype(jnp.float32)
    summed = from_far + from_mid + grads[4 * TILE :].astype(jnp.float32)
    back = shifted(summed[:TILE].astype(jnp.bfloat16), -1).astype(jnp.float32)
    total = (summed[TILE:] + back).astype(jnp.bfloat16)
    return attended, query_grad, total[:, :HEAD], total[:, HEAD:]


def solution(mesh):
    rows = P(SEQ_AXES, "tp")
    return jax.shard_map(
        per_device,
        mesh=mesh,
        in_specs=(rows, rows, rows, rows, P()),
        out_specs=(rows, rows, rows, rows),
        check_vma=False,
    )
```

time: 146 us -> 61.3 us (0.42); the launches traced: 143 us -> 60.9 us
  local copies, waits for them, and re-layouts: 47.4 us -> 3.53 us
  other arithmetic: 24.5 us -> 0.08 us
  matrix products: 24.4 us -> 0 us
  waiting for transfers between devices: 1.53 us -> 22 us
  starting transfers between devices: 43 us -> 23.1 us
  Pallas kernels: 0 us -> 11.4 us
    dynamic_slice x36 -> x0, local copies, waits for them, and re-layouts: 27.4 us -> none  [the longest x18 13.7 us: tile_data(): kpos_tile = lax.dynamic_slice_in_dim(key_pos, start_offset, BLOCK_TOKENS, 0)]
    dot_general x42 -> x0, matrix products: 24.4 us -> none  [the longest x12 8.23 us: tile_data(): jnp.einsum('qhgd,khd->hgqk', query_block, key_tile, preferred_element_typ...]
    ppermute x10 -> x6, waiting for transfers between devices: 1.53 us -> 22 us  [shifted(): return lax.ppermute(block, SEQ_AXES, route)]
    ppermute x10 -> x6, starting transfers between devices: 43 us -> 23.1 us  [shifted(): return lax.ppermute(block, SEQ_AXES, route)]
    and x18 -> x0, other arithmetic: 12.9 us -> none  [tile_data(): (qdoc_block[:, None] == kdoc_tile[None, :]) & (kpos_tile[None, :] <= qpos...]
    pallas_call x0 -> x1, Pallas kernels: none -> 11.4 us  [attention(): pl.pallas_call(kernel, out_shape=(jax.ShapeDtypeStruct(q.shape, jnp.bfloa...]
    unnamed x21 -> x9, local copies, waits for them, and re-layouts: 9.81 us -> 2.86 us
    while x30 -> x0, local copies, waits for them, and re-layouts: 6.44 us -> none
  transfers between devices with their start and end apart: 10 -> 6, of which waited for: 1 -> 4; matrix products, arithmetic and copies ran while one was open for 9% -> 0% of each run, Pallas kernels for 0% -> 0%
where the time goes in v1:
time: 61.3 us; the launch traced here: 60.9 us
  starting transfers between devices  23.1 us (38%)
  waiting for transfers between devices  22 us (36%)
  Pallas kernels  11.4 us (19%)
  local copies, waits for them, and re-layouts  3.53 us (6%)
  between operations  0.75 us (1%)
    ppermute x6, starting transfers between devices, shifted(): return lax.ppermute(block, SEQ_AXES, route)  23.1 us
    ppermute x6, waiting for transfers between devices, shifted(): return lax.ppermute(block, SEQ_AXES, route)  22 us
    pallas_call x1, Pallas kernels, attention(): pl.pallas_call(kernel, out_shape=(jax.ShapeDtypeStruct(q.shape, jnp.bfloa...  11.4 us
    unnamed x9, local copies, waits for them, and re-layouts  2.86 us
  transfers between devices with their start and end apart: 6, of which 4 were waited for; matrix products, arithmetic and copies ran while one was open for 0% of the time, Pallas kernels for 0%

profile of v1, /device:TPU:1, one launch (start us, length us, event | category | flops | bytes accessed | tf_op | source)
XLA Modules:
  0.0 60.9 jit_solution(14136766793018209526)
XLA Ops:
  0.6 0.0 copy-start.3
  0.6 0.8 %constant_dynamic-update-slice_fusion.1 = bf16[128,256]{1,0:T(8,128)(2,1)S(1)} fusion(bf16[128,128]{1,0:T(8,128)(2,1)} %param.6), kind=kLoop, calls=%fused_computation.6 | loop fusion | bytes 65536
  1.4 0.0 copy-done.3
  1.4 3.9 %collective-permute-start = (bf16[128,256]{1,0:T(8,128)(2,1)S(1)}, bf16[128,256]{1,0:T(8,128)(2,1)S(1)}, u32[]{:S(2)}, u32[]{:S(2)}) collective-permute-start(bf16[128,256]{1,0:T(8,128)(2,1)S(1)} %constant_dynamic-update-slice_fusion), channel_id=1, source_target_pairs={{0,8},{8,16},{16,24},{24,32},{32,40},{40,48},{48,56},{56,64},{64,7... | collective-permute-start | bytes 196616 | tf_op jit(solution)/shard_map/ppermute | solution.py:28
  5.4 12.2 %collective-permute-done = bf16[128,256]{1,0:T(8,128)(2,1)S(1)} collective-permute-done((bf16[128,256]{1,0:T(8,128)(2,1)S(1)}, bf16[128,256]{1,0:T(8,128)(2,1)S(1)}, u32[]{:S(2)}, u32[]{:S(2)}) %collective-permute-start) | collective-permute-done | bytes 65568 | tf_op jit(solution)/shard_map/ppermute | solution.py:28
  17.6 1.9 %collective-permute-start.2 = (bf16[256,256]{1,0:T(8,128)(2,1)S(1)}, bf16[256,256]{1,0:T(8,128)(2,1)S(1)}, u32[]{:S(2)}, u32[]{:S(2)}) collective-permute-start(bf16[256,256]{1,0:T(8,128)(2,1)S(1)} %pad_maximum_fusion.near_ref), channel_id=1, source_target_pairs={{0,16},{8,24},{16,32},{24,40},{32,48},{40,56},{48,64},{56,72},{64,... | collective-permute-start | bytes 393224 | tf_op jit(solution)/shard_map/ppermute | solution.py:28
  19.6 1.9 %collective-permute-start.1 = (bf16[256,256]{1,0:T(8,128)(2,1)S(1)}, bf16[256,256]{1,0:T(8,128)(2,1)S(1)}, u32[]{:S(2)}, u32[]{:S(2)}) collective-permute-start(bf16[256,256]{1,0:T(8,128)(2,1)S(1)} %pad_maximum_fusion.near_ref), channel_id=1, source_target_pairs={{0,32},{8,40},{16,48},{24,56},{32,64},{40,72},{48,80},{56,88},{64,... | collective-permute-start | bytes 393224 | tf_op jit(solution)/shard_map/ppermute | solution.py:28
  21.5 0.0 copy-start.2
  21.5 6.0 %collective-permute-done.2.mid_ref = bf16[256,256]{1,0:T(8,128)(2,1)S(1)} collective-permute-done((bf16[256,256]{1,0:T(8,128)(2,1)S(1)}, bf16[256,256]{1,0:T(8,128)(2,1)S(1)}, u32[]{:S(2)}, u32[]{:S(2)}) %collective-permute-start.2) | collective-permute-done | bytes 131104 | tf_op jit(solution)/shard_map/ppermute | solution.py:28
  27.5 0.0 collective-permute-done.1.far_ref
  27.5 0.0 copy-done.2
  27.6 0.0 copy-start
  27.6 1.0 %copy-done = bf16[128,2048]{1,0:T(8,128)(2,1)S(1)} copy-done((bf16[128,2048]{1,0:T(8,128)(2,1)S(1)}, bf16[128,2048]{1,0:T(8,128)(2,1)}, u32[]{:S(2)}) %copy-start) | copy-done | bytes 524312
  28.6 0.0 copy-start.1
  28.6 1.0 %copy-done.1 = bf16[128,2048]{1,0:T(8,128)(2,1)S(1)} copy-done((bf16[128,2048]{1,0:T(8,128)(2,1)S(1)}, bf16[128,2048]{1,0:T(8,128)(2,1)}, u32[]{:S(2)}) %copy-start.1) | copy-done | bytes 524312
  29.6 11.4 %shard_map.84 = (bf16[128,2048]{1,0:T(8,128)(2,1)}, bf16[128,2048]{1,0:T(8,128)(2,1)}, bf16[768,256]{1,0:T(8,128)(2,1)S(1)}) custom-call(s32[32]{0:T(128)S(1)} %copy-done.2, s32[1]{0:T(128)} %bitcast.index_ref, bf16[128,2048]{1,0:T(8,128)(2,1)S(1)} %copy-done, bf16[128,2048]{1,0:T(8,128)(2,1)S(1)} %copy-done.1, ...), custom_call_target="tpu_custom_call" | custom-call | flops 2415919104 | bytes 2883584 | tf_op jit(solution)/shard_map/pallas_call | solution.py:95
  41.1 4.5 %collective-permute-start.3 = (bf16[256,256]{1,0:T(8,128)(2,1)S(1)}, bf16[256,256]{1,0:T(8,128)(2,1)S(1)}, u32[]{:S(2)}, u32[]{:S(2)}) collective-permute-start(bf16[256,256]{1,0:T(8,128)(2,1)S(1)} %get-tuple-element.10), channel_id=1, source_target_pairs={{32,0},{40,8},{48,16},{56,24},{64,32},{72,40},{80,48},{88,56},{96,... | collective-permute-start | bytes 393224 | tf_op jit(solution)/shard_map/ppermute | solution.py:28
  45.7 4.8 %collective-permute-start.4 = (bf16[256,256]{1,0:T(8,128)(2,1)S(1)}, bf16[256,256]{1,0:T(8,128)(2,1)S(1)}, u32[]{:S(2)}, u32[]{:S(2)}) collective-permute-start(bf16[256,256]{1,0:T(8,128)(2,1)S(1)} %get-tuple-element.11), channel_id=1, source_target_pairs={{16,0},{24,8},{32,16},{40,24},{48,32},{56,40},{64,48},{72,56},{80,... | collective-permute-start | bytes 393224 | tf_op jit(solution)/shard_map/ppermute | solution.py:28
  50.5 0.0 collective-permute-done.3
  50.5 2.4 %collective-permute-done.4 = bf16[256,256]{1,0:T(8,128)(2,1)S(1)} collective-permute-done((bf16[256,256]{1,0:T(8,128)(2,1)S(1)}, bf16[256,256]{1,0:T(8,128)(2,1)S(1)}, u32[]{:S(2)}, u32[]{:S(2)}) %collective-permute-start.4) | collective-permute-done | bytes 131104 | tf_op jit(solution)/shard_map/ppermute | solution.py:28
  52.9 0.1 convert_add_fusion
  53.0 6.0 %collective-permute-start.5 = (bf16[128,256]{1,0:T(8,128)(2,1)S(1)}, bf16[128,256]{1,0:T(8,128)(2,1)S(1)}, u32[]{:S(2)}, u32[]{:S(2)}) collective-permute-start(bf16[128,256]{1,0:T(8,128)(2,1)S(1)} %slice.38), channel_id=1, source_target_pairs={{8,0},{16,8},{24,16},{32,24},{40,32},{48,40},{56,48},{64,56},{72,6... | collective-permute-start | bytes 196616 | tf_op jit(solution)/shard_map/ppermute | solution.py:28
  59.0 1.3 %collective-permute-done.5 = bf16[128,256]{1,0:T(8,128)(2,1)S(1)} collective-permute-done((bf16[128,256]{1,0:T(8,128)(2,1)S(1)}, bf16[128,256]{1,0:T(8,128)(2,1)S(1)}, u32[]{:S(2)}, u32[]{:S(2)}) %collective-permute-start.5) | collective-permute-done | bytes 65568 | tf_op jit(solution)/shard_map/ppermute | solution.py:28
  60.3 0.6 %fusion.2 = (bf16[128,128]{1,0:T(8,128)(2,1)}, bf16[128,128]{1,0:T(8,128)(2,1)}) fusion(bf16[128,256]{1,0:T(8,128)(2,1)S(1)} %fusion), kind=kLoop, calls=%fused_computation.8 | loop fusion | bytes 131072 | tf_op jit(solution)/shard_map/slice | solution.py:137
  (5 shorter events, 0.1 us)
Async XLA Ops:
  0.6 0.8 %copy-start.3 = (bf16[128,128]{1,0:T(8,128)(2,1)S(1)}, bf16[128,128]{1,0:T(8,128)(2,1)}, u32[]{:S(2)}) copy-start(bf16[128,128]{1,0:T(8,128)(2,1)} %param.7) | copy-start | bytes 98308
  1.4 16.2 %collective-permute-start = (bf16[128,256]{1,0:T(8,128)(2,1)S(1)}, bf16[128,256]{1,0:T(8,128)(2,1)S(1)}, u32[]{:S(2)}, u32[]{:S(2)}) collective-permute-start(bf16[128,256]{1,0:T(8,128)(2,1)S(1)} %constant_dynamic-update-slice_fusion), channel_id=1, source_target_pairs={{0,8},{8,16},{16,24},{24,32},{32,40},{40,48},{48,56},{56,64},{64,7... | collective-permute-start | bytes 196616 | tf_op jit(solution)/shard_map/ppermute | solution.py:28
  17.6 9.9 %collective-permute-start.2 = (bf16[256,256]{1,0:T(8,128)(2,1)S(1)}, bf16[256,256]{1,0:T(8,128)(2,1)S(1)}, u32[]{:S(2)}, u32[]{:S(2)}) collective-permute-start(bf16[256,256]{1,0:T(8,128)(2,1)S(1)} %pad_maximum_fusion.near_ref), channel_id=1, source_target_pairs={{0,16},{8,24},{16,32},{24,40},{32,48},{40,56},{48,64},{56,72},{64,... | collective-permute-start | bytes 393224 | tf_op jit(solution)/shard_map/ppermute | solution.py:28
  19.6 8.0 %collective-permute-start.1 = (bf16[256,256]{1,0:T(8,128)(2,1)S(1)}, bf16[256,256]{1,0:T(8,128)(2,1)S(1)}, u32[]{:S(2)}, u32[]{:S(2)}) collective-permute-start(bf16[256,256]{1,0:T(8,128)(2,1)S(1)} %pad_maximum_fusion.near_ref), channel_id=1, source_target_pairs={{0,32},{8,40},{16,48},{24,56},{32,64},{40,72},{48,80},{56,88},{64,... | collective-permute-start | bytes 393224 | tf_op jit(solution)/shard_map/ppermute | solution.py:28
  21.5 6.0 %copy-start.2 = (s32[32]{0:T(128)S(1)}, s32[32]{0:T(128)}, u32[]{:S(2)}) copy-start(s32[32]{0:T(128)} %lens_ref.1) | copy-start | bytes 388
  27.6 1.0 %copy-start = (bf16[128,2048]{1,0:T(8,128)(2,1)S(1)}, bf16[128,2048]{1,0:T(8,128)(2,1)}, u32[]{:S(2)}) copy-start(bf16[128,2048]{1,0:T(8,128)(2,1)} %q_ref.1) | copy-start | bytes 1572868
  28.6 1.0 %copy-start.1 = (bf16[128,2048]{1,0:T(8,128)(2,1)S(1)}, bf16[128,2048]{1,0:T(8,128)(2,1)}, u32[]{:S(2)}) copy-start(bf16[128,2048]{1,0:T(8,128)(2,1)} %do_ref.1) | copy-start | bytes 1572868
  41.1 9.4 %collective-permute-start.3 = (bf16[256,256]{1,0:T(8,128)(2,1)S(1)}, bf16[256,256]{1,0:T(8,128)(2,1)S(1)}, u32[]{:S(2)}, u32[]{:S(2)}) collective-permute-start(bf16[256,256]{1,0:T(8,128)(2,1)S(1)} %get-tuple-element.10), channel_id=1, source_target_pairs={{32,0},{40,8},{48,16},{56,24},{64,32},{72,40},{80,48},{88,56},{96,... | collective-permute-start | bytes 393224 | tf_op jit(solution)/shard_map/ppermute | solution.py:28
  45.7 7.2 %collective-permute-start.4 = (bf16[256,256]{1,0:T(8,128)(2,1)S(1)}, bf16[256,256]{1,0:T(8,128)(2,1)S(1)}, u32[]{:S(2)}, u32[]{:S(2)}) collective-permute-start(bf16[256,256]{1,0:T(8,128)(2,1)S(1)} %get-tuple-element.11), channel_id=1, source_target_pairs={{16,0},{24,8},{32,16},{40,24},{48,32},{56,40},{64,48},{72,56},{80,... | collective-permute-start | bytes 393224 | tf_op jit(solution)/shard_map/ppermute | solution.py:28
  53.0 7.3 %collective-permute-start.5 = (bf16[128,256]{1,0:T(8,128)(2,1)S(1)}, bf16[128,256]{1,0:T(8,128)(2,1)S(1)}, u32[]{:S(2)}, u32[]{:S(2)}) collective-permute-start(bf16[128,256]{1,0:T(8,128)(2,1)S(1)} %slice.38), channel_id=1, source_target_pairs={{8,0},{16,8},{24,16},{32,24},{40,32},{48,40},{56,48},{64,56},{72,6... | collective-permute-start | bytes 196616 | tf_op jit(solution)/shard_map/ppermute | solution.py:28

commit v2 on v1

v2 whole, which is shorter than its diff:
```python
import functools

import jax
import jax.numpy as jnp
from jax import lax
from jax.experimental import pallas as pl
from jax.experimental.pallas import tpu as pltpu
from jax.sharding import PartitionSpec as P

HEAD = 128
TILE = 128
REACH = 5
SPAN = (REACH + 1) * TILE
CHUNK = 2 * TILE
SEQ_AXES = ("dp", "ctx")
SCALE = HEAD ** (-0.5)
LOG2E = 1.4426950408889634
NEG = -1e30
STEP = 2 * TILE

NT = (((1,), (1,)), ((), ()))
NN = (((1,), (0,)), ((), ()))
BF16 = jnp.bfloat16
F32 = jnp.float32


def dot(a, b, dims):
    return lax.dot_general(a, b, dims, preferred_element_type=F32)


def shifted(block, distance):
    devices = range(lax.axis_size(SEQ_AXES))
    route = [(i - distance, i) for i in devices if i - distance in devices]
    return lax.ppermute(block, SEQ_AXES, route)


def twice(x):
    return jnp.concatenate([x, x], 1)


def stack_kernel(
    lens_ref, index_ref, q_ref, do_ref, qs_ref, dos_ref, bias_ref, sems
):
    copies = []
    for h in range(q_ref.shape[1] // HEAD):
        part = pl.ds(h * HEAD, HEAD)
        for x, (src, dst) in enumerate(((q_ref, qs_ref), (do_ref, dos_ref))):
            copies.append(
                pltpu.make_async_copy(src.at[:, part], dst.at[part, :], sems.at[x, h])
            )
            copies[-1].start()
    base = (index_ref[0] - REACH) * TILE
    q_pos = base + REACH * TILE + lax.broadcasted_iota(jnp.int32, (8, TILE), 1)
    doc_start = jnp.zeros((8, TILE), jnp.int32)
    end = jnp.int32(0)
    for i in range(lens_ref.shape[0]):
        end = end + lens_ref[i]
        doc_start = jnp.where(q_pos >= end, jnp.maximum(doc_start, end), doc_start)
    q_pos, doc_start = q_pos[:1], doc_start[:1]
    for t in range(REACH + 1):
        k_pos = base + t * TILE + lax.broadcasted_iota(jnp.int32, (TILE, TILE), 0)
        seen = (k_pos >= doc_start) & (k_pos <= q_pos)
        bias_ref[pl.ds(t * TILE, TILE), :] = jnp.where(seen, 0.0, NEG)
    for copy in copies:
        copy.wait()


def scores(qs_ref, dos_ref, kv_ref, bias_ref, at, part):
    dp = dot(kv_ref[:, HEAD:], dos_ref[part, :], NT)
    s = dot(kv_ref[:, :HEAD], qs_ref[part, :], NT) * (SCALE * LOG2E)
    s = s + twice(bias_ref[pl.ds(at * CHUNK, CHUNK), :])
    m = jnp.max(s, axis=0, keepdims=True)
    e = jnp.exp2(s - m)
    total = jnp.sum(e, axis=0, keepdims=True)
    return e, dp, m, total, jnp.sum(e * dp, axis=0, keepdims=True)


def parts_of(qs_ref):
    return [pl.ds(j * STEP, STEP) for j in range(qs_ref.shape[0] // STEP)]


def score_kernel(at, qs_ref, dos_ref, kv_ref, bias_ref, e_ref, dp_ref, stats_ref):
    for part in parts_of(qs_ref):
        e, dp, m, total, delta = scores(qs_ref, dos_ref, kv_ref, bias_ref, at, part)
        e_ref[:, part] = e
        dp_ref[:, part] = dp
        stats_ref[0:1, part] = m
        stats_ref[1:2, part] = total
        stats_ref[2:3, part] = delta


def grads(qs_ref, dos_ref, w_ref, ds_ref, out_ref):
    out_ref[:, :HEAD] = (dot(ds_ref[...], qs_ref[...], NN) * SCALE).astype(out_ref.dtype)
    out_ref[:, HEAD:] = dot(w_ref[...], dos_ref[...], NN).astype(out_ref.dtype)


def last_kernel(
    at, qs_ref, dos_ref, kv_ref, bias_ref, one_ref, two_ref,
    w_ref, ds_ref, stats_ref, out_ref,
):
    for part in parts_of(qs_ref):
        e, dp, m, total, delta = scores(qs_ref, dos_ref, kv_ref, bias_ref, at, part)
        m_one, m_two = one_ref[0:1, part], two_ref[0:1, part]
        top = jnp.maximum(m, jnp.maximum(m_one, m_two))
        a, a_one, a_two = (jnp.exp2(x - top) for x in (m, m_one, m_two))
        total = a * total + a_one * one_ref[1:2, part] + a_two * two_ref[1:2, part]
        delta = a * delta + a_one * one_ref[2:3, part] + a_two * two_ref[2:3, part]
        r = 1.0 / total
        delta = delta * r
        p = e * (a * r)
        w_ref[:, part] = p.astype(BF16)
        ds_ref[:, part] = (p * (dp - delta)).astype(BF16)
        stats_ref[0:1, part] = a_one * r
        stats_ref[1:2, part] = a_two * r
        stats_ref[2:3, part] = delta
    grads(qs_ref, dos_ref, w_ref, ds_ref, out_ref)


def grad_kernel(row, qs_ref, dos_ref, e_ref, dp_ref, stats_ref, w_ref, ds_ref, out_ref):
    for part in parts_of(qs_ref):
        p = e_ref[:, part] * stats_ref[row : row + 1, part]
        w_ref[:, part] = p.astype(BF16)
        ds_ref[:, part] = (p * (dp_ref[:, part] - stats_ref[2:3, part])).astype(BF16)
    grads(qs_ref, dos_ref, w_ref, ds_ref, out_ref)


def query_kernel(far_ref, mid_ref, near_ref, *refs):
    ws, dss, (o_ref, dq_ref, t_ref) = refs[:3], refs[3:6], refs[6:]
    for t, ref in enumerate((far_ref, mid_ref, near_ref)):
        t_ref[:, pl.ds(t * CHUNK, CHUNK)] = ref[...].T
    for j, part in enumerate(pl.ds(j * STEP, STEP) for j in range(ws[0].shape[1] // STEP)):
        w = jnp.concatenate([ref[:, part] for ref in ws], 0)
        ds = jnp.concatenate([ref[:, part] for ref in dss], 0)
        o = dot(t_ref[HEAD:, :], w, NN).astype(BF16)
        dq = (dot(t_ref[:HEAD, :], ds, NN) * SCALE).astype(BF16)
        for x, ref in ((o, o_ref), (dq, dq_ref)):
            ref[:, pl.ds(j * STEP, HEAD)] = x[:, :TILE].T
            ref[:, pl.ds(j * STEP + HEAD, HEAD)] = x[:, TILE:].T


def call(kernel, args, outs, flops=0, scratch=(), spaces=None, limit=16):
    vmem = pl.BlockSpec(memory_space=pltpu.VMEM)
    specs = [pl.BlockSpec(memory_space=s) for s in spaces or [pltpu.VMEM] * len(args)]
    outs = tuple(jax.ShapeDtypeStruct(shape, dtype) for shape, dtype in outs)
    size = sum(x.size * x.dtype.itemsize for x in list(args) + list(outs))
    return pl.pallas_call(
        kernel,
        out_shape=outs,
        in_specs=specs,
        out_specs=(vmem,) * len(outs),
        scratch_shapes=list(scratch),
        compiler_params=pltpu.CompilerParams(vmem_limit_bytes=limit << 20),
        cost_estimate=pl.CostEstimate(flops=flops, transcendentals=0, bytes_accessed=size),
    )(*args)


def prepare(lens, index, q, do):
    n = q.shape[0] * q.shape[1] // HEAD
    q, do = (pltpu.with_memory_space_constraint(x, pltpu.HBM) for x in (q, do))
    return call(
        stack_kernel, (lens, index, q, do),
        (((n, HEAD), BF16), ((n, HEAD), BF16), ((SPAN, TILE), F32)),
        spaces=[pltpu.SMEM, pltpu.SMEM, pltpu.HBM, pltpu.HBM],
        scratch=(pltpu.SemaphoreType.DMA((2, q.shape[1] // HEAD)),),
    )


def score_part(at, qs, dos, kv, bias):
    n = qs.shape[0]
    return call(
        functools.partial(score_kernel, at), (qs, dos, kv, bias),
        (((CHUNK, n), F32), ((CHUNK, n), F32), ((8, n), F32)), 4 * CHUNK * n * HEAD,
    )


def last_part(at, qs, dos, kv, bias, one, two):
    n = qs.shape[0]
    return call(
        functools.partial(last_kernel, at), (qs, dos, kv, bias, one, two),
        (((CHUNK, n), BF16), ((CHUNK, n), BF16), ((8, n), F32), ((CHUNK, 2 * HEAD), BF16)),
        8 * CHUNK * n * HEAD,
    )


def grad_part(row, qs, dos, e, dp, stats, dtype):
    n = qs.shape[0]
    return call(
        functools.partial(grad_kernel, row), (qs, dos, e, dp, stats),
        (((CHUNK, n), BF16), ((CHUNK, n), BF16), ((CHUNK, 2 * HEAD), dtype)),
        4 * CHUNK * n * HEAD,
    )


def query_part(kvs, ws, dss, shape):
    n = ws[0].shape[1]
    return call(
        query_kernel, (*kvs, *ws, *dss), ((shape, BF16), (shape, BF16)),
        4 * SPAN * n * HEAD, scratch=(pltpu.VMEM((2 * HEAD, SPAN), BF16),),
    )


def per_device(queries, keys, values, output_gradient, doc_lens):
    index = lax.axis_index(SEQ_AXES).astype(jnp.int32).reshape(1)
    own = jnp.concatenate([keys, values], 1)
    before = shifted(own, 1)
    qs, dos, bias = prepare(doc_lens, index, queries, output_gradient)
    before, bias = lax.optimization_barrier((before, bias))
    near = jnp.concatenate([before, own], 0)
    mid = shifted(near, 2)
    far = shifted(near, 4)
    e_near, dp_near, st_near = score_part(2, qs, dos, near, bias)
    e_mid, dp_mid, st_mid = score_part(1, qs, dos, mid, bias)
    w_far, ds_far, stats, g_far = last_part(0, qs, dos, far, bias, st_near, st_mid)
    from_far = shifted(g_far, -4)
    w_mid, ds_mid, g_mid = grad_part(1, qs, dos, e_mid, dp_mid, stats, BF16)
    from_mid = shifted(g_mid, -2)
    w_near, ds_near, g_near = grad_part(0, qs, dos, e_near, dp_near, stats, F32)
    summed = from_far.astype(F32) + from_mid.astype(F32) + g_near
    back = shifted(summed[:TILE].astype(BF16), -1).astype(F32)
    attended, query_grad = query_part(
        (far, mid, near), (w_far, w_mid, w_near), (ds_far, ds_mid, ds_near), queries.shape
    )
    total = (summed[TILE:] + back).astype(BF16)
    return attended, query_grad, total[:, :HEAD], total[:, HEAD:]


def bench(lens, index, q, do, far, mid, near):
    qs, dos, bias = prepare(lens, index, q, do)
    e_near, dp_near, st_near = score_part(2, qs, dos, near, bias)
    e_mid, dp_mid, st_mid = score_part(1, qs, dos, mid, bias)
    w_far, ds_far, stats, g_far = last_part(0, qs, dos, far, bias, st_near, st_mid)
    w_mid, ds_mid, g_mid = grad_part(1, qs, dos, e_mid, dp_mid, stats, BF16)
    w_near, ds_near, g_near = grad_part(0, qs, dos, e_near, dp_near, stats, F32)
    o, dq = query_part(
        (far, mid, near), (w_far, w_mid, w_near), (ds_far, ds_mid, ds_near), q.shape
    )
    return o, dq, jnp.concatenate([g_far.astype(F32), g_mid.astype(F32), g_near], 0)


def solution(mesh):
    rows = P(SEQ_AXES, "tp")
    return jax.shard_map(
        per_device,
        mesh=mesh,
        in_specs=(rows, rows, rows, rows, P()),
        out_specs=(rows, rows, rows, rows),
        check_vma=False,
    )
```

time: 61.3 us -> 52.3 us (0.85)
  waiting for transfers between devices: 22 us -> 17.2 us
  starting transfers between devices: 23.1 us -> 21.2 us
  Pallas kernels: 11.4 us -> 9.81 us
  local copies, waits for them, and re-layouts: 3.53 us -> 2.83 us
    ppermute x6, waiting for transfers between devices: 22 us -> 17.2 us  [shifted(): return lax.ppermute(block, SEQ_AXES, route)]
    ppermute x6, starting transfers between devices: 23.1 us -> 21.2 us  [shifted(): return lax.ppermute(block, SEQ_AXES, route)]
    pallas_call x1 -> x7, Pallas kernels: 11.4 us -> 9.81 us  [call(): pl.pallas_call(kernel, out_shape=outs, in_specs=specs, out_specs=(vmem,)...]
    unnamed x9 -> x3, local copies, waits for them, and re-layouts: 2.86 us -> 1.42 us
    concatenate x1, local copies, waits for them, and re-layouts: 0.01 us -> 0.77 us  [per_device(): own = jnp.concatenate([keys, values], 1)]
  transfers between devices with their start and end apart: 6 -> 6, of which waited for: 4 -> 3; matrix products, arithmetic and copies ran while one was open for 0% -> 0% of each run, Pallas kernels for 0% -> 15%
where the time goes in v2:
time: 52.3 us; the launch traced here: 51.9 us
  starting transfers between devices  21.2 us (41%)
  waiting for transfers between devices  17.2 us (33%)
  Pallas kernels  9.81 us (19%)
  local copies, waits for them, and re-layouts  2.83 us (5%)
  between operations  0.77 us (1%)
    ppermute x6, starting transfers between devices, shifted(): return lax.ppermute(block, SEQ_AXES, route)  21.2 us
    ppermute x6, waiting for transfers between devices, shifted(): return lax.ppermute(block, SEQ_AXES, route)  17.2 us
    pallas_call x7, Pallas kernels, call(): pl.pallas_call(kernel, out_shape=outs, in_specs=specs, out_specs=(vmem,)...  9.81 us
    unnamed x3, local copies, waits for them, and re-layouts  1.42 us
  transfers between devices with their start and end apart: 6, of which 3 were waited for; matrix products, arithmetic and copies ran while one was open for 0% of the time, Pallas kernels for 15%

profile of v2, /device:TPU:1, one launch (start us, length us, event | category | flops | bytes accessed | tf_op | source)
XLA Modules:
  0.0 51.9 jit_solution(9600479355455460872)
XLA Ops:
  0.6 0.8 %constant_dynamic-update-slice_fusion.1 = bf16[128,256]{1,0:T(8,128)(2,1)S(1)} fusion(bf16[128,128]{1,0:T(8,128)(2,1)} %param.6), kind=kLoop, calls=%fused_computation.6 | loop fusion | bytes 65536
  1.4 0.8 %constant_dynamic-update-slice_fusion = bf16[128,256]{1,0:T(8,128)(2,1)S(1)} fusion(bf16[128,256]{1,0:T(8,128)(2,1)S(1)} %constant_dynamic-update-slice_fusion.1, bf16[128,128]{1,0:T(8,128)(2,1)} %param.7), kind=kLoop, calls=%fused_computation.5 | loop fusion | bytes 65536 | tf_op jit(solution)/shard_map/concatenate | solution.py:204
  2.2 3.9 %collective-permute-start = (bf16[128,256]{1,0:T(8,128)(2,1)S(1)}, bf16[128,256]{1,0:T(8,128)(2,1)S(1)}, u32[]{:S(2)}, u32[]{:S(2)}) collective-permute-start(bf16[128,256]{1,0:T(8,128)(2,1)S(1)} %constant_dynamic-update-slice_fusion), channel_id=1, source_target_pairs={{0,8},{8,16},{16,24},{24,32},{32,40},{40,48},{48,56},{56,64},{64,7... | collective-permute-start | bytes 196616 | tf_op jit(solution)/shard_map/ppermute | solution.py:34
  6.1 0.0 copy-start
  6.1 0.6 %copy-done = s32[32]{0:T(128)S(1)} copy-done((s32[32]{0:T(128)S(1)}, s32[32]{0:T(128)}, u32[]{:S(2)}) %copy-start) | copy-done | bytes 152
  6.8 2.0 %shard_map.84 = (bf16[2048,128]{1,0:T(8,128)(2,1)S(1)}, bf16[2048,128]{1,0:T(8,128)(2,1)S(1)}, f32[768,128]{1,0:T(8,128)S(1)}) custom-call(s32[32]{0:T(128)S(1)} %copy-done, s32[1]{0:T(128)} %bitcast.index_ref, bf16[128,2048]{1,0:T(8,128)(2,1)} %q_ref.1, bf16[128,2048]{1,0:T(8,128)(2,1)} %do_ref.1), custom_call_target="tpu_custom_call" | custom-call | bytes 2490500 | tf_op jit(solution)/shard_map/pallas_call | solution.py:146
  8.8 9.6 %collective-permute-done = bf16[128,256]{1,0:T(8,128)(2,1)S(1)} collective-permute-done((bf16[128,256]{1,0:T(8,128)(2,1)S(1)}, bf16[128,256]{1,0:T(8,128)(2,1)S(1)}, u32[]{:S(2)}, u32[]{:S(2)}) %collective-permute-start) | collective-permute-done | bytes 65568 | tf_op jit(solution)/shard_map/ppermute | solution.py:34
  18.4 1.9 %collective-permute-start.2 = (bf16[256,256]{1,0:T(8,128)(2,1)S(1)}, bf16[256,256]{1,0:T(8,128)(2,1)S(1)}, u32[]{:S(2)}, u32[]{:S(2)}) collective-permute-start(bf16[256,256]{1,0:T(8,128)(2,1)S(1)} %pad_maximum_fusion.kv_ref.near_ref), channel_id=1, source_target_pairs={{0,16},{8,24},{16,32},{24,40},{32,48},{40,56},{48,64},{56,72},{64,... | collective-permute-start | bytes 393224 | tf_op jit(solution)/shard_map/ppermute | solution.py:34
  20.3 1.9 %collective-permute-start.1 = (bf16[256,256]{1,0:T(8,128)(2,1)S(1)}, bf16[256,256]{1,0:T(8,128)(2,1)S(1)}, u32[]{:S(2)}, u32[]{:S(2)}) collective-permute-start(bf16[256,256]{1,0:T(8,128)(2,1)S(1)} %pad_maximum_fusion.kv_ref.near_ref), channel_id=1, source_target_pairs={{0,32},{8,40},{16,48},{24,56},{32,64},{40,72},{48,80},{56,88},{64,... | collective-permute-start | bytes 393224 | tf_op jit(solution)/shard_map/ppermute | solution.py:34
  22.2 1.0 %shard_map.85 = (f32[256,2048]{1,0:T(8,128)S(1)}, f32[256,2048]{1,0:T(8,128)S(1)}, f32[8,2048]{1,0:T(8,128)S(1)}) custom-call(bf16[2048,128]{1,0:T(8,128)(2,1)S(1)} %get-tuple-element.29.qs_ref, bf16[2048,128]{1,0:T(8,128)(2,1)S(1)} %get-tuple-element.30.dos_ref, bf16[256,256]{1,0:T(8,128)(2,1)S(1)} %pad_maximum_fusion.kv_ref.near_ref, ...), custom_call_target="tpu_custom_call" | custom-call | flops 268435456 | bytes 5832704 | tf_op jit(solution)/shard_map/pallas_call | solution.py:146
  23.2 5.1 %collective-permute-done.2.kv_ref.mid_ref = bf16[256,256]{1,0:T(8,128)(2,1)S(1)} collective-permute-done((bf16[256,256]{1,0:T(8,128)(2,1)S(1)}, bf16[256,256]{1,0:T(8,128)(2,1)S(1)}, u32[]{:S(2)}, u32[]{:S(2)}) %collective-permute-start.2) | collective-permute-done | bytes 131104 | tf_op jit(solution)/shard_map/ppermute | solution.py:34
  28.3 1.0 %shard_map.86 = (f32[256,2048]{1,0:T(8,128)S(1)}, f32[256,2048]{1,0:T(8,128)S(1)}, f32[8,2048]{1,0:T(8,128)S(1)}) custom-call(bf16[2048,128]{1,0:T(8,128)(2,1)S(1)} %get-tuple-element.29.qs_ref, bf16[2048,128]{1,0:T(8,128)(2,1)S(1)} %get-tuple-element.30.dos_ref, bf16[256,256]{1,0:T(8,128)(2,1)S(1)} %collective-permute-done.2.kv_ref.mid_ref, ...), custom_call_target="tpu_custom_call" | custom-call | flops 268435456 | bytes 5832704 | tf_op jit(solution)/shard_map/pallas_call | solution.py:146
  29.2 0.0 collective-permute-done.1.kv_ref.far_ref
  29.2 2.2 %shard_map.87 = (bf16[256,2048]{1,0:T(8,128)(2,1)S(1)}, bf16[256,2048]{1,0:T(8,128)(2,1)S(1)}, f32[8,2048]{1,0:T(8,128)S(1)}, bf16[256,256]{1,0:T(8,128)(2,1)S(1)}) custom-call(bf16[2048,128]{1,0:T(8,128)(2,1)S(1)} %get-tuple-element.29.qs_ref, bf16[2048,128]{1,0:T(8,128)(2,1)S(1)} %get-tuple-element.30.dos_ref, ...), custom_call_target="tpu_custom_call" | custom-call | flops 536870912 | bytes 3997696 | tf_op jit(solution)/shard_map/pallas_call | solution.py:146
  31.5 4.5 %collective-permute-start.3 = (bf16[256,256]{1,0:T(8,128)(2,1)S(1)}, bf16[256,256]{1,0:T(8,128)(2,1)S(1)}, u32[]{:S(2)}, u32[]{:S(2)}) collective-permute-start(bf16[256,256]{1,0:T(8,128)(2,1)S(1)} %get-tuple-element.47), channel_id=1, source_target_pairs={{32,0},{40,8},{48,16},{56,24},{64,32},{72,40},{80,48},{88,56},{96,... | collective-permute-start | bytes 393224 | tf_op jit(solution)/shard_map/ppermute | solution.py:34
  36.0 0.8 %shard_map.88 = (bf16[256,2048]{1,0:T(8,128)(2,1)S(1)}, bf16[256,2048]{1,0:T(8,128)(2,1)S(1)}, bf16[256,256]{1,0:T(8,128)(2,1)S(1)}) custom-call(bf16[2048,128]{1,0:T(8,128)(2,1)S(1)} %get-tuple-element.29.qs_ref, bf16[2048,128]{1,0:T(8,128)(2,1)S(1)} %get-tuple-element.30.dos_ref, f32[256,2048]{1,0:T(8,128)S(1)} %get-tuple-element.35.e_ref, ...), custom_call_target="tpu_custom_call" | custom-call | flops 268435456 | bytes 7536640 | tf_op jit(solution)/shard_map/pallas_call | solution.py:146
  36.8 3.8 %collective-permute-start.4 = (bf16[256,256]{1,0:T(8,128)(2,1)S(1)}, bf16[256,256]{1,0:T(8,128)(2,1)S(1)}, u32[]{:S(2)}, u32[]{:S(2)}) collective-permute-start(bf16[256,256]{1,0:T(8,128)(2,1)S(1)} %get-tuple-element.48), channel_id=1, source_target_pairs={{16,0},{24,8},{32,16},{40,24},{48,32},{56,40},{64,48},{72,56},{80,... | collective-permute-start | bytes 393224 | tf_op jit(solution)/shard_map/ppermute | solution.py:34
  40.7 0.8 %shard_map.89 = (bf16[256,2048]{1,0:T(8,128)(2,1)S(1)}, bf16[256,2048]{1,0:T(8,128)(2,1)S(1)}, f32[256,256]{1,0:T(8,128)S(1)}) custom-call(bf16[2048,128]{1,0:T(8,128)(2,1)S(1)} %get-tuple-element.29.qs_ref, bf16[2048,128]{1,0:T(8,128)(2,1)S(1)} %get-tuple-element.30.dos_ref, f32[256,2048]{1,0:T(8,128)S(1)} %get-tuple-element.39.e_ref, ...), custom_call_target="tpu_custom_call" | custom-call | flops 268435456 | bytes 7667712 | tf_op jit(solution)/shard_map/pallas_call | solution.py:146
  41.5 0.0 collective-permute-done.3
  41.5 2.6 %collective-permute-done.4 = bf16[256,256]{1,0:T(8,128)(2,1)S(1)} collective-permute-done((bf16[256,256]{1,0:T(8,128)(2,1)S(1)}, bf16[256,256]{1,0:T(8,128)(2,1)S(1)}, u32[]{:S(2)}, u32[]{:S(2)}) %collective-permute-start.4) | collective-permute-done | bytes 131104 | tf_op jit(solution)/shard_map/ppermute | solution.py:34
  44.1 5.0 %collective-permute-start.5 = (bf16[128,256]{1,0:T(8,128)(2,1)S(1)}, bf16[128,256]{1,0:T(8,128)(2,1)S(1)}, u32[]{:S(2)}, u32[]{:S(2)}) collective-permute-start(bf16[128,256]{1,0:T(8,128)(2,1)S(1)} %slice.25), channel_id=1, source_target_pairs={{8,0},{16,8},{24,16},{32,24},{40,32},{48,40},{56,48},{64,56},{72,6... | collective-permute-start | bytes 196616 | tf_op jit(solution)/shard_map/ppermute | solution.py:34
  49.1 2.1 %shard_map.90 = (bf16[128,2048]{1,0:T(8,128)(2,1)}, bf16[128,2048]{1,0:T(8,128)(2,1)}) custom-call(bf16[256,256]{1,0:T(8,128)(2,1)S(1)} %collective-permute-done.1.kv_ref.far_ref, bf16[256,256]{1,0:T(8,128)(2,1)S(1)} %collective-permute-done.2.kv_ref.mid_ref, bf16[256,256]{1,0:T(8,128)(2,1)S(1)} %pad_maximum_fusion.kv_ref.near_ref, ...), custom_call_target="tpu_custom_call" | custom-call | flops 805306368 | bytes 7733248 | tf_op jit(solution)/shard_map/pallas_call | solution.py:146
  51.2 0.0 collective-permute-done.5
  51.2 0.6 %fusion.1 = (bf16[128,128]{1,0:T(8,128)(2,1)}, bf16[128,128]{1,0:T(8,128)(2,1)}) fusion(bf16[128,256]{1,0:T(8,128)(2,1)S(1)} %fusion), kind=kLoop, calls=%fused_computation.7 | loop fusion | bytes 131072 | tf_op jit(solution)/shard_map/slice | solution.py:224
  (4 shorter events, 0.1 us)
Async XLA Ops:
  2.2 16.2 %collective-permute-start = (bf16[128,256]{1,0:T(8,128)(2,1)S(1)}, bf16[128,256]{1,0:T(8,128)(2,1)S(1)}, u32[]{:S(2)}, u32[]{:S(2)}) collective-permute-start(bf16[128,256]{1,0:T(8,128)(2,1)S(1)} %constant_dynamic-update-slice_fusion), channel_id=1, source_target_pairs={{0,8},{8,16},{16,24},{24,32},{32,40},{40,48},{48,56},{56,64},{64,7... | collective-permute-start | bytes 196616 | tf_op jit(solution)/shard_map/ppermute | solution.py:34
  6.1 0.7 %copy-start = (s32[32]{0:T(128)S(1)}, s32[32]{0:T(128)}, u32[]{:S(2)}) copy-start(s32[32]{0:T(128)} %lens_ref.1) | copy-start | bytes 388
  18.4 9.9 %collective-permute-start.2 = (bf16[256,256]{1,0:T(8,128)(2,1)S(1)}, bf16[256,256]{1,0:T(8,128)(2,1)S(1)}, u32[]{:S(2)}, u32[]{:S(2)}) collective-permute-start(bf16[256,256]{1,0:T(8,128)(2,1)S(1)} %pad_maximum_fusion.kv_ref.near_ref), channel_id=1, source_target_pairs={{0,16},{8,24},{16,32},{24,40},{32,48},{40,56},{48,64},{56,72},{64,... | collective-permute-start | bytes 393224 | tf_op jit(solution)/shard_map/ppermute | solution.py:34
  20.3 8.9 %collective-permute-start.1 = (bf16[256,256]{1,0:T(8,128)(2,1)S(1)}, bf16[256,256]{1,0:T(8,128)(2,1)S(1)}, u32[]{:S(2)}, u32[]{:S(2)}) collective-permute-start(bf16[256,256]{1,0:T(8,128)(2,1)S(1)} %pad_maximum_fusion.kv_ref.near_ref), channel_id=1, source_target_pairs={{0,32},{8,40},{16,48},{24,56},{32,64},{40,72},{48,80},{56,88},{64,... | collective-permute-start | bytes 393224 | tf_op jit(solution)/shard_map/ppermute | solution.py:34
  31.5 10.0 %collective-permute-start.3 = (bf16[256,256]{1,0:T(8,128)(2,1)S(1)}, bf16[256,256]{1,0:T(8,128)(2,1)S(1)}, u32[]{:S(2)}, u32[]{:S(2)}) collective-permute-start(bf16[256,256]{1,0:T(8,128)(2,1)S(1)} %get-tuple-element.47), channel_id=1, source_target_pairs={{32,0},{40,8},{48,16},{56,24},{64,32},{72,40},{80,48},{88,56},{96,... | collective-permute-start | bytes 393224 | tf_op jit(solution)/shard_map/ppermute | solution.py:34
  36.8 7.2 %collective-permute-start.4 = (bf16[256,256]{1,0:T(8,128)(2,1)S(1)}, bf16[256,256]{1,0:T(8,128)(2,1)S(1)}, u32[]{:S(2)}, u32[]{:S(2)}) collective-permute-start(bf16[256,256]{1,0:T(8,128)(2,1)S(1)} %get-tuple-element.48), channel_id=1, source_target_pairs={{16,0},{24,8},{32,16},{40,24},{48,32},{56,40},{64,48},{72,56},{80,... | collective-permute-start | bytes 393224 | tf_op jit(solution)/shard_map/ppermute | solution.py:34
  44.1 7.1 %collective-permute-start.5 = (bf16[128,256]{1,0:T(8,128)(2,1)S(1)}, bf16[128,256]{1,0:T(8,128)(2,1)S(1)}, u32[]{:S(2)}, u32[]{:S(2)}) collective-permute-start(bf16[128,256]{1,0:T(8,128)(2,1)S(1)} %slice.25), channel_id=1, source_target_pairs={{8,0},{16,8},{24,16},{32,24},{40,32},{48,40},{56,48},{64,56},{72,6... | collective-permute-start | bytes 196616 | tf_op jit(solution)/shard_map/ppermute | solution.py:34

commit v3 on v2

--- a/solution.py
+++ b/solution.py
@@ -17,6 +17,7 @@
 LOG2E = 1.4426950408889634
 NEG = -1e30
 STEP = 2 * TILE
+KEY, VALUE = pl.ds(0, HEAD), pl.ds(HEAD, HEAD)
 
 NT = (((1,), (1,)), ((), ()))
 NN = (((1,), (0,)), ((), ()))
@@ -165,6 +166,25 @@
     )
 
 
+def join_kernel(k_ref, v_ref, out_ref, sems):
+    copies = [
+        pltpu.make_async_copy(k_ref, out_ref.at[:, KEY], sems.at[0]),
+        pltpu.make_async_copy(v_ref, out_ref.at[:, VALUE], sems.at[1]),
+    ]
+    for copy in copies:
+        copy.start()
+    for copy in copies:
+        copy.wait()
+
+
+def join(k, v):
+    k, v = (pltpu.with_memory_space_constraint(x, pltpu.HBM) for x in (k, v))
+    return call(
+        join_kernel, (k, v), (((k.shape[0], 2 * HEAD), BF16),), spaces=[pltpu.HBM] * 2,
+        scratch=(pltpu.SemaphoreType.DMA((2,)),),
+    )[0]
+
+
 def score_part(at, qs, dos, kv, bias):
     n = qs.shape[0]
     return call(
@@ -201,7 +221,7 @@
 
 def per_device(queries, keys, values, output_gradient, doc_lens):
     index = lax.axis_index(SEQ_AXES).astype(jnp.int32).reshape(1)
-    own = jnp.concatenate([keys, values], 1)
+    own = join(keys, values)
     before = shifted(own, 1)
     qs, dos, bias = prepare(doc_lens, index, queries, output_gradient)
     before, bias = lax.optimization_barrier((before, bias))
@@ -209,32 +229,22 @@
     mid = shifted(near, 2)
     far = shifted(near, 4)
     e_near, dp_near, st_near = score_part(2, qs, dos, near, bias)
-    e_mid, dp_mid, st_mid = score_part(1, qs, dos, mid, bias)
-    w_far, ds_far, stats, g_far = last_part(0, qs, dos, far, bias, st_near, st_mid)
+    e_far, dp_far, st_far = score_part(0, qs, dos, far, bias)
+    w_mid, ds_mid, stats, g_mid = last_part(1, qs, dos, mid, bias, st_near, st_far)
+    from_mid = shifted(g_mid, -2)
+    w_far, ds_far, g_far = grad_part(1, qs, dos, e_far, dp_far, stats, BF16)
     from_far = shifted(g_far, -4)
-    w_mid, ds_mid, g_mid = grad_part(1, qs, dos, e_mid, dp_mid, stats, BF16)
-    from_mid = shifted(g_mid, -2)
     w_near, ds_near, g_near = grad_part(0, qs, dos, e_near, dp_near, stats, F32)
+    attended, query_grad = query_part(
+        (far, mid, near), (w_far, w_mid, w_near), (ds_far, ds_mid, ds_near), queries.shape
+    )
+    attended, query_grad, from_far, from_mid = lax.optimization_barrier(
+        (attended, query_grad, from_far, from_mid)
+    )
     summed = from_far.astype(F32) + from_mid.astype(F32) + g_near
     back = shifted(summed[:TILE].astype(BF16), -1).astype(F32)
-    attended, query_grad = query_part(
-        (far, mid, near), (w_far, w_mid, w_near), (ds_far, ds_mid, ds_near), queries.shape
-    )
     total = (summed[TILE:] + back).astype(BF16)
     return attended, query_grad, total[:, :HEAD], total[:, HEAD:]
-
-
-def bench(lens, index, q, do, far, mid, near):
-    qs, dos, bias = prepare(lens, index, q, do)
-    e_near, dp_near, st_near = score_part(2, qs, dos, near, bias)
-    e_mid, dp_mid, st_mid = score_part(1, qs, dos, mid, bias)
-    w_far, ds_far, stats, g_far = last_part(0, qs, dos, far, bias, st_near, st_mid)
-    w_mid, ds_mid, g_mid = grad_part(1, qs, dos, e_mid, dp_mid, stats, BF16)
-    w_near, ds_near, g_near = grad_part(0, qs, dos, e_near, dp_near, stats, F32)
-    o, dq = query_part(
-        (far, mid, near), (w_far, w_mid, w_near), (ds_far, ds_mid, ds_near), q.shape
-    )
-    return o, dq, jnp.concatenate([g_far.astype(F32), g_mid.astype(F32), g_near], 0)
 
 
 def solution(mesh):

time: 52.3 us -> 49.4 us (0.945)
  starting transfers between devices: 21.2 us -> 19.3 us
  local copies, waits for them, and re-layouts: 2.83 us -> 1.29 us
  Pallas kernels: 9.81 us -> 10.6 us
    ppermute x6, starting transfers between devices: 21.2 us -> 19.3 us  [shifted(): return lax.ppermute(block, SEQ_AXES, route)]
    pallas_call x7 -> x8, Pallas kernels: 9.81 us -> 10.6 us  [call(): pl.pallas_call(kernel, out_shape=outs, in_specs=specs, out_specs=(vmem,)...]
    concatenate x1 -> x0, local copies, waits for them, and re-layouts: 0.77 us -> none  [per_device(): own = jnp.concatenate([keys, values], 1)]
    unnamed x3 -> x2, local copies, waits for them, and re-layouts: 1.42 us -> 0.65 us
  transfers between devices with their start and end apart: 6 -> 6, of which waited for: 3 -> 4; matrix products, arithmetic and copies ran while one was open for 0% -> 0% of each run, Pallas kernels for 15% -> 15%
where the time goes in v3:
time: 49.4 us; the launch traced here: 49 us
  starting transfers between devices  19.3 us (39%)
  waiting for transfers between devices  16.9 us (34%)
  Pallas kernels  10.6 us (21%)
  local copies, waits for them, and re-layouts  1.29 us (3%)
  between operations  0.76 us (2%)
    ppermute x6, starting transfers between devices, shifted(): return lax.ppermute(block, SEQ_AXES, route)  19.3 us
    ppermute x6, waiting for transfers between devices, shifted(): return lax.ppermute(block, SEQ_AXES, route)  16.9 us
    pallas_call x8, Pallas kernels, call(): pl.pallas_call(kernel, out_shape=outs, in_specs=specs, out_specs=(vmem,)...  10.6 us
  transfers between devices with their start and end apart: 6, of which 4 were waited for; matrix products, arithmetic and copies ran while one was open for 0% of the time, Pallas kernels for 15%

profile of v3, /device:TPU:1, one launch (start us, length us, event | category | flops | bytes accessed | tf_op | source)
XLA Modules:
  0.0 49.0 jit_solution(2757984938750983988)
XLA Ops:
  0.6 0.8 %shard_map.84 = bf16[128,256]{1,0:T(8,128)(2,1)S(1)} custom-call(bf16[128,128]{1,0:T(8,128)(2,1)} %k_ref.1, bf16[128,128]{1,0:T(8,128)(2,1)} %v_ref.1), custom_call_target="tpu_custom_call" | custom-call | bytes 131072 | tf_op jit(solution)/shard_map/pallas_call | solution.py:147
  1.4 3.9 %collective-permute-start = (bf16[128,256]{1,0:T(8,128)(2,1)S(1)}, bf16[128,256]{1,0:T(8,128)(2,1)S(1)}, u32[]{:S(2)}, u32[]{:S(2)}) collective-permute-start(bf16[128,256]{1,0:T(8,128)(2,1)S(1)} %shard_map.84), channel_id=1, source_target_pairs={{0,8},{8,16},{16,24},{24,32},{32,40},{40,48},{48,56},{56,64},{64,7... | collective-permute-start | bytes 196616 | tf_op jit(solution)/shard_map/ppermute | solution.py:35
  5.4 0.0 copy-start
  5.4 0.6 %copy-done = s32[32]{0:T(128)S(1)} copy-done((s32[32]{0:T(128)S(1)}, s32[32]{0:T(128)}, u32[]{:S(2)}) %copy-start) | copy-done | bytes 152
  6.1 2.0 %shard_map.85 = (bf16[2048,128]{1,0:T(8,128)(2,1)S(1)}, bf16[2048,128]{1,0:T(8,128)(2,1)S(1)}, f32[768,128]{1,0:T(8,128)S(1)}) custom-call(s32[32]{0:T(128)S(1)} %copy-done, s32[1]{0:T(128)} %bitcast.index_ref, bf16[128,2048]{1,0:T(8,128)(2,1)} %q_ref.1, bf16[128,2048]{1,0:T(8,128)(2,1)} %do_ref.1), custom_call_target="tpu_custom_call" | custom-call | bytes 2490500 | tf_op jit(solution)/shard_map/pallas_call | solution.py:147
  8.1 9.6 %collective-permute-done = bf16[128,256]{1,0:T(8,128)(2,1)S(1)} collective-permute-done((bf16[128,256]{1,0:T(8,128)(2,1)S(1)}, bf16[128,256]{1,0:T(8,128)(2,1)S(1)}, u32[]{:S(2)}, u32[]{:S(2)}) %collective-permute-start) | collective-permute-done | bytes 65568 | tf_op jit(solution)/shard_map/ppermute | solution.py:35
  17.6 1.9 %collective-permute-start.1 = (bf16[256,256]{1,0:T(8,128)(2,1)S(1)}, bf16[256,256]{1,0:T(8,128)(2,1)S(1)}, u32[]{:S(2)}, u32[]{:S(2)}) collective-permute-start(bf16[256,256]{1,0:T(8,128)(2,1)S(1)} %pad_maximum_fusion.kv_ref.near_ref), channel_id=1, source_target_pairs={{0,32},{8,40},{16,48},{24,56},{32,64},{40,72},{48,80},{56,88},{64,... | collective-permute-start | bytes 393224 | tf_op jit(solution)/shard_map/ppermute | solution.py:35
  19.6 1.9 %collective-permute-start.2 = (bf16[256,256]{1,0:T(8,128)(2,1)S(1)}, bf16[256,256]{1,0:T(8,128)(2,1)S(1)}, u32[]{:S(2)}, u32[]{:S(2)}) collective-permute-start(bf16[256,256]{1,0:T(8,128)(2,1)S(1)} %pad_maximum_fusion.kv_ref.near_ref), channel_id=1, source_target_pairs={{0,16},{8,24},{16,32},{24,40},{32,48},{40,56},{48,64},{56,72},{64,... | collective-permute-start | bytes 393224 | tf_op jit(solution)/shard_map/ppermute | solution.py:35
  21.5 1.0 %shard_map.87 = (f32[256,2048]{1,0:T(8,128)S(1)}, f32[256,2048]{1,0:T(8,128)S(1)}, f32[8,2048]{1,0:T(8,128)S(1)}) custom-call(bf16[2048,128]{1,0:T(8,128)(2,1)S(1)} %get-tuple-element.33.qs_ref, bf16[2048,128]{1,0:T(8,128)(2,1)S(1)} %get-tuple-element.34.dos_ref, bf16[256,256]{1,0:T(8,128)(2,1)S(1)} %pad_maximum_fusion.kv_ref.near_ref, ...), custom_call_target="tpu_custom_call" | custom-call | flops 268435456 | bytes 5832704 | tf_op jit(solution)/shard_map/pallas_call | solution.py:147
  22.5 2.7 %collective-permute-done.1.kv_ref.far_ref = bf16[256,256]{1,0:T(8,128)(2,1)S(1)} collective-permute-done((bf16[256,256]{1,0:T(8,128)(2,1)S(1)}, bf16[256,256]{1,0:T(8,128)(2,1)S(1)}, u32[]{:S(2)}, u32[]{:S(2)}) %collective-permute-start.1) | collective-permute-done | bytes 131104 | tf_op jit(solution)/shard_map/ppermute | solution.py:35
  25.1 1.0 %shard_map.86 = (f32[256,2048]{1,0:T(8,128)S(1)}, f32[256,2048]{1,0:T(8,128)S(1)}, f32[8,2048]{1,0:T(8,128)S(1)}) custom-call(bf16[2048,128]{1,0:T(8,128)(2,1)S(1)} %get-tuple-element.33.qs_ref, bf16[2048,128]{1,0:T(8,128)(2,1)S(1)} %get-tuple-element.34.dos_ref, bf16[256,256]{1,0:T(8,128)(2,1)S(1)} %collective-permute-done.1.kv_ref.far_ref, ...), custom_call_target="tpu_custom_call" | custom-call | flops 268435456 | bytes 5832704 | tf_op jit(solution)/shard_map/pallas_call | solution.py:147
  26.1 3.4 %collective-permute-done.2.kv_ref.mid_ref = bf16[256,256]{1,0:T(8,128)(2,1)S(1)} collective-permute-done((bf16[256,256]{1,0:T(8,128)(2,1)S(1)}, bf16[256,256]{1,0:T(8,128)(2,1)S(1)}, u32[]{:S(2)}, u32[]{:S(2)}) %collective-permute-start.2) | collective-permute-done | bytes 131104 | tf_op jit(solution)/shard_map/ppermute | solution.py:35
  29.5 2.2 %shard_map.88 = (bf16[256,2048]{1,0:T(8,128)(2,1)S(1)}, bf16[256,2048]{1,0:T(8,128)(2,1)S(1)}, f32[8,2048]{1,0:T(8,128)S(1)}, bf16[256,256]{1,0:T(8,128)(2,1)S(1)}) custom-call(bf16[2048,128]{1,0:T(8,128)(2,1)S(1)} %get-tuple-element.33.qs_ref, bf16[2048,128]{1,0:T(8,128)(2,1)S(1)} %get-tuple-element.34.dos_ref, ...), custom_call_target="tpu_custom_call" | custom-call | flops 536870912 | bytes 3997696 | tf_op jit(solution)/shard_map/pallas_call | solution.py:147
  31.7 3.0 %collective-permute-start.4 = (bf16[256,256]{1,0:T(8,128)(2,1)S(1)}, bf16[256,256]{1,0:T(8,128)(2,1)S(1)}, u32[]{:S(2)}, u32[]{:S(2)}) collective-permute-start(bf16[256,256]{1,0:T(8,128)(2,1)S(1)} %get-tuple-element.52), channel_id=1, source_target_pairs={{16,0},{24,8},{32,16},{40,24},{48,32},{56,40},{64,48},{72,56},{80,... | collective-permute-start | bytes 393224 | tf_op jit(solution)/shard_map/ppermute | solution.py:35
  34.7 0.8 %shard_map.89 = (bf16[256,2048]{1,0:T(8,128)(2,1)S(1)}, bf16[256,2048]{1,0:T(8,128)(2,1)S(1)}, bf16[256,256]{1,0:T(8,128)(2,1)S(1)}) custom-call(bf16[2048,128]{1,0:T(8,128)(2,1)S(1)} %get-tuple-element.33.qs_ref, bf16[2048,128]{1,0:T(8,128)(2,1)S(1)} %get-tuple-element.34.dos_ref, f32[256,2048]{1,0:T(8,128)S(1)} %get-tuple-element.36.e_ref, ...), custom_call_target="tpu_custom_call" | custom-call | flops 268435456 | bytes 7536640 | tf_op jit(solution)/shard_map/pallas_call | solution.py:147
  35.5 3.9 %collective-permute-start.3 = (bf16[256,256]{1,0:T(8,128)(2,1)S(1)}, bf16[256,256]{1,0:T(8,128)(2,1)S(1)}, u32[]{:S(2)}, u32[]{:S(2)}) collective-permute-start(bf16[256,256]{1,0:T(8,128)(2,1)S(1)} %get-tuple-element.51), channel_id=1, source_target_pairs={{32,0},{40,8},{48,16},{56,24},{64,32},{72,40},{80,48},{88,56},{96,... | collective-permute-start | bytes 393224 | tf_op jit(solution)/shard_map/ppermute | solution.py:35
  39.4 0.8 %shard_map.90 = (bf16[256,2048]{1,0:T(8,128)(2,1)S(1)}, bf16[256,2048]{1,0:T(8,128)(2,1)S(1)}, f32[256,256]{1,0:T(8,128)S(1)}) custom-call(bf16[2048,128]{1,0:T(8,128)(2,1)S(1)} %get-tuple-element.33.qs_ref, bf16[2048,128]{1,0:T(8,128)(2,1)S(1)} %get-tuple-element.34.dos_ref, f32[256,2048]{1,0:T(8,128)S(1)} %get-tuple-element.43.e_ref, ...), custom_call_target="tpu_custom_call" | custom-call | flops 268435456 | bytes 7667712 | tf_op jit(solution)/shard_map/pallas_call | solution.py:147
  40.2 2.1 %shard_map.91 = (bf16[128,2048]{1,0:T(8,128)(2,1)}, bf16[128,2048]{1,0:T(8,128)(2,1)}) custom-call(bf16[256,256]{1,0:T(8,128)(2,1)S(1)} %collective-permute-done.1.kv_ref.far_ref, bf16[256,256]{1,0:T(8,128)(2,1)S(1)} %collective-permute-done.2.kv_ref.mid_ref, bf16[256,256]{1,0:T(8,128)(2,1)S(1)} %pad_maximum_fusion.kv_ref.near_ref, ...), custom_call_target="tpu_custom_call" | custom-call | flops 805306368 | bytes 7733248 | tf_op jit(solution)/shard_map/pallas_call | solution.py:147
  42.3 0.0 collective-permute-done.4
  42.3 0.0 collective-permute-done.3
  42.3 4.7 %collective-permute-start.5 = (bf16[128,256]{1,0:T(8,128)(2,1)S(1)}, bf16[128,256]{1,0:T(8,128)(2,1)S(1)}, u32[]{:S(2)}, u32[]{:S(2)}) collective-permute-start(bf16[128,256]{1,0:T(8,128)(2,1)S(1)} %slice.25), channel_id=1, source_target_pairs={{8,0},{16,8},{24,16},{32,24},{40,32},{48,40},{56,48},{64,56},{72,6... | collective-permute-start | bytes 196616 | tf_op jit(solution)/shard_map/ppermute | solution.py:35
  47.0 1.3 %collective-permute-done.5 = bf16[128,256]{1,0:T(8,128)(2,1)S(1)} collective-permute-done((bf16[128,256]{1,0:T(8,128)(2,1)S(1)}, bf16[128,256]{1,0:T(8,128)(2,1)S(1)}, u32[]{:S(2)}, u32[]{:S(2)}) %collective-permute-start.5) | collective-permute-done | bytes 65568 | tf_op jit(solution)/shard_map/ppermute | solution.py:35
  48.3 0.6 %fusion.1 = (bf16[128,128]{1,0:T(8,128)(2,1)}, bf16[128,128]{1,0:T(8,128)(2,1)}) fusion(bf16[128,256]{1,0:T(8,128)(2,1)S(1)} %fusion), kind=kLoop, calls=%fused_computation.5 | loop fusion | bytes 131072 | tf_op jit(solution)/shard_map/slice | solution.py:247
  (4 shorter events, 0.1 us)
Async XLA Ops:
  1.4 16.2 %collective-permute-start = (bf16[128,256]{1,0:T(8,128)(2,1)S(1)}, bf16[128,256]{1,0:T(8,128)(2,1)S(1)}, u32[]{:S(2)}, u32[]{:S(2)}) collective-permute-start(bf16[128,256]{1,0:T(8,128)(2,1)S(1)} %shard_map.84), channel_id=1, source_target_pairs={{0,8},{8,16},{16,24},{24,32},{32,40},{40,48},{48,56},{56,64},{64,7... | collective-permute-start | bytes 196616 | tf_op jit(solution)/shard_map/ppermute | solution.py:35
  5.4 0.7 %copy-start = (s32[32]{0:T(128)S(1)}, s32[32]{0:T(128)}, u32[]{:S(2)}) copy-start(s32[32]{0:T(128)} %lens_ref.1) | copy-start | bytes 388
  17.6 7.5 %collective-permute-start.1 = (bf16[256,256]{1,0:T(8,128)(2,1)S(1)}, bf16[256,256]{1,0:T(8,128)(2,1)S(1)}, u32[]{:S(2)}, u32[]{:S(2)}) collective-permute-start(bf16[256,256]{1,0:T(8,128)(2,1)S(1)} %pad_maximum_fusion.kv_ref.near_ref), channel_id=1, source_target_pairs={{0,32},{8,40},{16,48},{24,56},{32,64},{40,72},{48,80},{56,88},{64,... | collective-permute-start | bytes 393224 | tf_op jit(solution)/shard_map/ppermute | solution.py:35
  19.6 9.9 %collective-permute-start.2 = (bf16[256,256]{1,0:T(8,128)(2,1)S(1)}, bf16[256,256]{1,0:T(8,128)(2,1)S(1)}, u32[]{:S(2)}, u32[]{:S(2)}) collective-permute-start(bf16[256,256]{1,0:T(8,128)(2,1)S(1)} %pad_maximum_fusion.kv_ref.near_ref), channel_id=1, source_target_pairs={{0,16},{8,24},{16,32},{24,40},{32,48},{40,56},{48,64},{56,72},{64,... | collective-permute-start | bytes 393224 | tf_op jit(solution)/shard_map/ppermute | solution.py:35
  31.7 10.6 %collective-permute-start.4 = (bf16[256,256]{1,0:T(8,128)(2,1)S(1)}, bf16[256,256]{1,0:T(8,128)(2,1)S(1)}, u32[]{:S(2)}, u32[]{:S(2)}) collective-permute-start(bf16[256,256]{1,0:T(8,128)(2,1)S(1)} %get-tuple-element.52), channel_id=1, source_target_pairs={{16,0},{24,8},{32,16},{40,24},{48,32},{56,40},{64,48},{72,56},{80,... | collective-permute-start | bytes 393224 | tf_op jit(solution)/shard_map/ppermute | solution.py:35
  35.5 6.8 %collective-permute-start.3 = (bf16[256,256]{1,0:T(8,128)(2,1)S(1)}, bf16[256,256]{1,0:T(8,128)(2,1)S(1)}, u32[]{:S(2)}, u32[]{:S(2)}) collective-permute-start(bf16[256,256]{1,0:T(8,128)(2,1)S(1)} %get-tuple-element.51), channel_id=1, source_target_pairs={{32,0},{40,8},{48,16},{56,24},{64,32},{72,40},{80,48},{88,56},{96,... | collective-permute-start | bytes 393224 | tf_op jit(solution)/shard_map/ppermute | solution.py:35
  42.3 6.0 %collective-permute-start.5 = (bf16[128,256]{1,0:T(8,128)(2,1)S(1)}, bf16[128,256]{1,0:T(8,128)(2,1)S(1)}, u32[]{:S(2)}, u32[]{:S(2)}) collective-permute-start(bf16[128,256]{1,0:T(8,128)(2,1)S(1)} %slice.25), channel_id=1, source_target_pairs={{8,0},{16,8},{24,16},{32,24},{40,32},{48,40},{56,48},{64,56},{72,6... | collective-permute-start | bytes 196616 | tf_op jit(solution)/shard_map/ppermute | solution.py:35

commit v4 on v3

--- a/solution.py
+++ b/solution.py
@@ -17,6 +17,7 @@
 LOG2E = 1.4426950408889634
 NEG = -1e30
 STEP = 2 * TILE
+PIECES = 4
 KEY, VALUE = pl.ds(0, HEAD), pl.ds(HEAD, HEAD)
 
 NT = (((1,), (1,)), ((), ()))
@@ -39,17 +40,20 @@
     return jnp.concatenate([x, x], 1)
 
 
-def stack_kernel(
-    lens_ref, index_ref, q_ref, do_ref, qs_ref, dos_ref, bias_ref, sems
+def prepare_kernel(
+    lens_hbm, index_ref, q_hbm, do_hbm, q_ref, do_ref, bias_ref, lens_ref, sems, lens_sem
 ):
+    lens = pltpu.make_async_copy(lens_hbm, lens_ref, lens_sem)
+    lens.start()
     copies = []
-    for h in range(q_ref.shape[1] // HEAD):
-        part = pl.ds(h * HEAD, HEAD)
-        for x, (src, dst) in enumerate(((q_ref, qs_ref), (do_ref, dos_ref))):
+    for c in range(PIECES):
+        rows = pl.ds(c * (TILE // PIECES), TILE // PIECES)
+        for x, (src, dst) in enumerate(((q_hbm, q_ref), (do_hbm, do_ref))):
             copies.append(
-                pltpu.make_async_copy(src.at[:, part], dst.at[part, :], sems.at[x, h])
+                pltpu.make_async_copy(src.at[rows, :], dst.at[rows, :], sems.at[x, c])
             )
             copies[-1].start()
+    lens.wait()
     base = (index_ref[0] - REACH) * TILE
     q_pos = base + REACH * TILE + lax.broadcasted_iota(jnp.int32, (8, TILE), 1)
     doc_start = jnp.zeros((8, TILE), jnp.int32)
@@ -66,9 +70,14 @@
         copy.wait()
 
 
+def stacked(ref, heads):
+    return jnp.concatenate([ref[:, pl.ds(h * HEAD, HEAD)] for h in heads], 0)
+
+
 def scores(qs_ref, dos_ref, kv_ref, bias_ref, at, part):
-    dp = dot(kv_ref[:, HEAD:], dos_ref[part, :], NT)
-    s = dot(kv_ref[:, :HEAD], qs_ref[part, :], NT) * (SCALE * LOG2E)
+    heads = (part.start // HEAD, part.start // HEAD + 1)
+    dp = dot(kv_ref[:, HEAD:], stacked(dos_ref, heads), NT)
+    s = dot(kv_ref[:, :HEAD], stacked(qs_ref, heads), NT) * (SCALE * LOG2E)
     s = s + twice(bias_ref[pl.ds(at * CHUNK, CHUNK), :])
     m = jnp.max(s, axis=0, keepdims=True)
     e = jnp.exp2(s - m)
@@ -77,7 +86,7 @@
 
 
 def parts_of(qs_ref):
-    return [pl.ds(j * STEP, STEP) for j in range(qs_ref.shape[0] // STEP)]
+    return [pl.ds(j * STEP, STEP) for j in range(qs_ref.shape[1] // STEP)]
 
 
 def score_kernel(at, qs_ref, dos_ref, kv_ref, bias_ref, e_ref, dp_ref, stats_ref):
@@ -91,37 +100,35 @@
 
 
 def grads(qs_ref, dos_ref, w_ref, ds_ref, out_ref):
-    out_ref[:, :HEAD] = (dot(ds_ref[...], qs_ref[...], NN) * SCALE).astype(out_ref.dtype)
-    out_ref[:, HEAD:] = dot(w_ref[...], dos_ref[...], NN).astype(out_ref.dtype)
+    heads = range(qs_ref.shape[1] // HEAD)
+    out_ref[:, :HEAD] = (dot(ds_ref[...], stacked(qs_ref, heads), NN) * SCALE).astype(out_ref.dtype)
+    out_ref[:, HEAD:] = dot(w_ref[...], stacked(dos_ref, heads), NN).astype(out_ref.dtype)
 
 
 def last_kernel(
-    at, qs_ref, dos_ref, kv_ref, bias_ref, one_ref, two_ref,
-    w_ref, ds_ref, stats_ref, out_ref,
+    at, qs_ref, dos_ref, kv_ref, bias_ref, one_ref, two_ref, e_ref, dp_ref, stats_ref
 ):
     for part in parts_of(qs_ref):
         e, dp, m, total, delta = scores(qs_ref, dos_ref, kv_ref, bias_ref, at, part)
+        e_ref[:, part] = e
+        dp_ref[:, part] = dp
         m_one, m_two = one_ref[0:1, part], two_ref[0:1, part]
         top = jnp.maximum(m, jnp.maximum(m_one, m_two))
         a, a_one, a_two = (jnp.exp2(x - top) for x in (m, m_one, m_two))
         total = a * total + a_one * one_ref[1:2, part] + a_two * two_ref[1:2, part]
         delta = a * delta + a_one * one_ref[2:3, part] + a_two * two_ref[2:3, part]
         r = 1.0 / total
-        delta = delta * r
-        p = e * (a * r)
-        w_ref[:, part] = p.astype(BF16)
-        ds_ref[:, part] = (p * (dp - delta)).astype(BF16)
         stats_ref[0:1, part] = a_one * r
         stats_ref[1:2, part] = a_two * r
-        stats_ref[2:3, part] = delta
-    grads(qs_ref, dos_ref, w_ref, ds_ref, out_ref)
+        stats_ref[2:3, part] = a * r
+        stats_ref[3:4, part] = delta * r
 
 
 def grad_kernel(row, qs_ref, dos_ref, e_ref, dp_ref, stats_ref, w_ref, ds_ref, out_ref):
     for part in parts_of(qs_ref):
         p = e_ref[:, part] * stats_ref[row : row + 1, part]
         w_ref[:, part] = p.astype(BF16)
-        ds_ref[:, part] = (p * (dp_ref[:, part] - stats_ref[2:3, part])).astype(BF16)
+        ds_ref[:, part] = (p * (dp_ref[:, part] - stats_ref[3:4, part])).astype(BF16)
     grads(qs_ref, dos_ref, w_ref, ds_ref, out_ref)
 
 
@@ -155,14 +162,21 @@
     )(*args)
 
 
+def in_hbm(*arrays):
+    return [pltpu.with_memory_space_constraint(x, pltpu.HBM) for x in arrays]
+
+
 def prepare(lens, index, q, do):
-    n = q.shape[0] * q.shape[1] // HEAD
-    q, do = (pltpu.with_memory_space_constraint(x, pltpu.HBM) for x in (q, do))
-    return call(
-        stack_kernel, (lens, index, q, do),
-        (((n, HEAD), BF16), ((n, HEAD), BF16), ((SPAN, TILE), F32)),
-        spaces=[pltpu.SMEM, pltpu.SMEM, pltpu.HBM, pltpu.HBM],
-        scratch=(pltpu.SemaphoreType.DMA((2, q.shape[1] // HEAD)),),
+    lens, q, do = in_hbm(lens, q, do)
+    return call(
+        prepare_kernel, (lens, index, q, do),
+        ((q.shape, BF16), (do.shape, BF16), ((SPAN, TILE), F32)),
+        spaces=[pltpu.HBM, pltpu.SMEM, pltpu.HBM, pltpu.HBM],
+        scratch=(
+            pltpu.SMEM(lens.shape, jnp.int32),
+            pltpu.SemaphoreType.DMA((2, PIECES)),
+            pltpu.SemaphoreType.DMA,
+        ),
     )
 
 
@@ -178,7 +192,7 @@
 
 
 def join(k, v):
-    k, v = (pltpu.with_memory_space_constraint(x, pltpu.HBM) for x in (k, v))
+    k, v = in_hbm(k, v)
     return call(
         join_kernel, (k, v), (((k.shape[0], 2 * HEAD), BF16),), spaces=[pltpu.HBM] * 2,
         scratch=(pltpu.SemaphoreType.DMA((2,)),),
@@ -186,7 +200,7 @@
 
 
 def score_part(at, qs, dos, kv, bias):
-    n = qs.shape[0]
+    n = qs.size // HEAD
     return call(
         functools.partial(score_kernel, at), (qs, dos, kv, bias),
         (((CHUNK, n), F32), ((CHUNK, n), F32), ((8, n), F32)), 4 * CHUNK * n * HEAD,
@@ -194,16 +208,15 @@
 
 
 def last_part(at, qs, dos, kv, bias, one, two):
-    n = qs.shape[0]
+    n = qs.size // HEAD
     return call(
         functools.partial(last_kernel, at), (qs, dos, kv, bias, one, two),
-        (((CHUNK, n), BF16), ((CHUNK, n), BF16), ((8, n), F32), ((CHUNK, 2 * HEAD), BF16)),
-        8 * CHUNK * n * HEAD,
+        (((CHUNK, n), F32), ((CHUNK, n), F32), ((8, n), F32)), 4 * CHUNK * n * HEAD,
     )
 
 
 def grad_part(row, qs, dos, e, dp, stats, dtype):
-    n = qs.shape[0]
+    n = qs.size // HEAD
     return call(
         functools.partial(grad_kernel, row), (qs, dos, e, dp, stats),
         (((CHUNK, n), BF16), ((CHUNK, n), BF16), ((CHUNK, 2 * HEAD), dtype)),
@@ -230,7 +243,8 @@
     far = shifted(near, 4)
     e_near, dp_near, st_near = score_part(2, qs, dos, near, bias)
     e_far, dp_far, st_far = score_part(0, qs, dos, far, bias)
-    w_mid, ds_mid, stats, g_mid = last_part(1, qs, dos, mid, bias, st_near, st_far)
+    e_mid, dp_mid, stats = last_part(1, qs, dos, mid, bias, st_near, st_far)
+    w_mid, ds_mid, g_mid = grad_part(2, qs, dos, e_mid, dp_mid, stats, BF16)
     from_mid = shifted(g_mid, -2)
     w_far, ds_far, g_far = grad_part(1, qs, dos, e_far, dp_far, stats, BF16)
     from_far = shifted(g_far, -4)

time: 49.4 us -> 49 us (level)
  waiting for transfers between devices: 16.9 us -> 18.2 us
  Pallas kernels: 10.6 us -> 9.74 us
  local copies, waits for them, and re-layouts: 1.29 us -> 0.64 us
    ppermute x6, waiting for transfers between devices: 16.9 us -> 18.2 us  [shifted(): return lax.ppermute(block, SEQ_AXES, route)]
    pallas_call x8 -> x9, Pallas kernels: 10.6 us -> 9.74 us  [call(): pl.pallas_call(kernel, out_shape=outs, in_specs=specs, out_specs=(vmem,)...]
    unnamed x2 -> x0, local copies, waits for them, and re-layouts: 0.65 us -> none
where the time goes in v4:
time: 49 us; the launch traced here: 48.6 us
  starting transfers between devices  19.3 us (39%)
  waiting for transfers between devices  18.2 us (37%)
  Pallas kernels  9.74 us (20%)
  between operations  0.76 us (2%)
  local copies, waits for them, and re-layouts  0.64 us (1%)
    ppermute x6, starting transfers between devices, shifted(): return lax.ppermute(block, SEQ_AXES, route)  19.3 us
    ppermute x6, waiting for transfers between devices, shifted(): return lax.ppermute(block, SEQ_AXES, route)  18.2 us
    pallas_call x9, Pallas kernels, call(): pl.pallas_call(kernel, out_shape=outs, in_specs=specs, out_specs=(vmem,)...  9.74 us
  transfers between devices with their start and end apart: 6, of which 4 were waited for; matrix products, arithmetic and copies ran while one was open for 0% of the time, Pallas kernels for 15%

profile of v4, /device:TPU:1, one launch (start us, length us, event | category | flops | bytes accessed | tf_op | source)
XLA Modules:
  0.0 48.6 jit_solution(12300054017910616226)
XLA Ops:
  0.6 0.8 %shard_map.84 = bf16[128,256]{1,0:T(8,128)(2,1)S(1)} custom-call(bf16[128,128]{1,0:T(8,128)(2,1)} %k_ref.1, bf16[128,128]{1,0:T(8,128)(2,1)} %v_ref.1), custom_call_target="tpu_custom_call" | custom-call | bytes 131072 | tf_op jit(solution)/shard_map/pallas_call | solution.py:154
  1.4 3.9 %collective-permute-start = (bf16[128,256]{1,0:T(8,128)(2,1)S(1)}, bf16[128,256]{1,0:T(8,128)(2,1)S(1)}, u32[]{:S(2)}, u32[]{:S(2)}) collective-permute-start(bf16[128,256]{1,0:T(8,128)(2,1)S(1)} %shard_map.84), channel_id=1, source_target_pairs={{0,8},{8,16},{16,24},{24,32},{32,40},{40,48},{48,56},{56,64},{64,7... | collective-permute-start | bytes 196616 | tf_op jit(solution)/shard_map/ppermute | solution.py:36
  5.4 1.4 %shard_map.85 = (bf16[128,2048]{1,0:T(8,128)(2,1)S(1)}, bf16[128,2048]{1,0:T(8,128)(2,1)S(1)}, f32[768,128]{1,0:T(8,128)S(1)}) custom-call(s32[32]{0:T(128)} %lens_hbm.1, s32[1]{0:T(128)} %bitcast.index_ref, bf16[128,2048]{1,0:T(8,128)(2,1)} %q_hbm.1, bf16[128,2048]{1,0:T(8,128)(2,1)} %do_hbm.1), custom_call_target="tpu_custom_call" | custom-call | bytes 2490500 | tf_op jit(solution)/shard_map/pallas_call | solution.py:154
  6.8 10.9 %collective-permute-done = bf16[128,256]{1,0:T(8,128)(2,1)S(1)} collective-permute-done((bf16[128,256]{1,0:T(8,128)(2,1)S(1)}, bf16[128,256]{1,0:T(8,128)(2,1)S(1)}, u32[]{:S(2)}, u32[]{:S(2)}) %collective-permute-start) | collective-permute-done | bytes 65568 | tf_op jit(solution)/shard_map/ppermute | solution.py:36
  17.6 1.9 %collective-permute-start.1 = (bf16[256,256]{1,0:T(8,128)(2,1)S(1)}, bf16[256,256]{1,0:T(8,128)(2,1)S(1)}, u32[]{:S(2)}, u32[]{:S(2)}) collective-permute-start(bf16[256,256]{1,0:T(8,128)(2,1)S(1)} %pad_maximum_fusion.kv_ref.near_ref), channel_id=1, source_target_pairs={{0,32},{8,40},{16,48},{24,56},{32,64},{40,72},{48,80},{56,88},{64,... | collective-permute-start | bytes 393224 | tf_op jit(solution)/shard_map/ppermute | solution.py:36
  19.6 1.9 %collective-permute-start.2 = (bf16[256,256]{1,0:T(8,128)(2,1)S(1)}, bf16[256,256]{1,0:T(8,128)(2,1)S(1)}, u32[]{:S(2)}, u32[]{:S(2)}) collective-permute-start(bf16[256,256]{1,0:T(8,128)(2,1)S(1)} %pad_maximum_fusion.kv_ref.near_ref), channel_id=1, source_target_pairs={{0,16},{8,24},{16,32},{24,40},{32,48},{40,56},{48,64},{56,72},{64,... | collective-permute-start | bytes 393224 | tf_op jit(solution)/shard_map/ppermute | solution.py:36
  21.5 1.0 %shard_map.87 = (f32[256,2048]{1,0:T(8,128)S(1)}, f32[256,2048]{1,0:T(8,128)S(1)}, f32[8,2048]{1,0:T(8,128)S(1)}) custom-call(bf16[128,2048]{1,0:T(8,128)(2,1)S(1)} %get-tuple-element.35.qs_ref, bf16[128,2048]{1,0:T(8,128)(2,1)S(1)} %get-tuple-element.36.dos_ref, bf16[256,256]{1,0:T(8,128)(2,1)S(1)} %pad_maximum_fusion.kv_ref.near_ref, ...), custom_call_target="tpu_custom_call" | custom-call | flops 268435456 | bytes 5832704 | tf_op jit(solution)/shard_map/pallas_call | solution.py:154
  22.5 2.6 %collective-permute-done.1.kv_ref.far_ref = bf16[256,256]{1,0:T(8,128)(2,1)S(1)} collective-permute-done((bf16[256,256]{1,0:T(8,128)(2,1)S(1)}, bf16[256,256]{1,0:T(8,128)(2,1)S(1)}, u32[]{:S(2)}, u32[]{:S(2)}) %collective-permute-start.1) | collective-permute-done | bytes 131104 | tf_op jit(solution)/shard_map/ppermute | solution.py:36
  25.1 1.0 %shard_map.86 = (f32[256,2048]{1,0:T(8,128)S(1)}, f32[256,2048]{1,0:T(8,128)S(1)}, f32[8,2048]{1,0:T(8,128)S(1)}) custom-call(bf16[128,2048]{1,0:T(8,128)(2,1)S(1)} %get-tuple-element.35.qs_ref, bf16[128,2048]{1,0:T(8,128)(2,1)S(1)} %get-tuple-element.36.dos_ref, bf16[256,256]{1,0:T(8,128)(2,1)S(1)} %collective-permute-done.1.kv_ref.far_ref, ...), custom_call_target="tpu_custom_call" | custom-call | flops 268435456 | bytes 5832704 | tf_op jit(solution)/shard_map/pallas_call | solution.py:154
  26.1 3.3 %collective-permute-done.2.kv_ref.mid_ref = bf16[256,256]{1,0:T(8,128)(2,1)S(1)} collective-permute-done((bf16[256,256]{1,0:T(8,128)(2,1)S(1)}, bf16[256,256]{1,0:T(8,128)(2,1)S(1)}, u32[]{:S(2)}, u32[]{:S(2)}) %collective-permute-start.2) | collective-permute-done | bytes 131104 | tf_op jit(solution)/shard_map/ppermute | solution.py:36
  29.5 1.0 %shard_map.88 = (f32[256,2048]{1,0:T(8,128)S(1)}, f32[256,2048]{1,0:T(8,128)S(1)}, f32[8,2048]{1,0:T(8,128)S(1)}) custom-call(bf16[128,2048]{1,0:T(8,128)(2,1)S(1)} %get-tuple-element.35.qs_ref, bf16[128,2048]{1,0:T(8,128)(2,1)S(1)} %get-tuple-element.36.dos_ref, bf16[256,256]{1,0:T(8,128)(2,1)S(1)} %collective-permute-done.2.kv_ref.mid_ref, ...), custom_call_target="tpu_custom_call" | custom-call | flops 268435456 | bytes 5963776 | tf_op jit(solution)/shard_map/pallas_call | solution.py:154
  30.5 0.8 %shard_map.90 = (bf16[256,2048]{1,0:T(8,128)(2,1)S(1)}, bf16[256,2048]{1,0:T(8,128)(2,1)S(1)}, bf16[256,256]{1,0:T(8,128)(2,1)S(1)}) custom-call(bf16[128,2048]{1,0:T(8,128)(2,1)S(1)} %get-tuple-element.35.qs_ref, bf16[128,2048]{1,0:T(8,128)(2,1)S(1)} %get-tuple-element.36.dos_ref, f32[256,2048]{1,0:T(8,128)S(1)} %get-tuple-element.44.e_ref, ...), custom_call_target="tpu_custom_call" | custom-call | flops 268435456 | bytes 7536640 | tf_op jit(solution)/shard_map/pallas_call | solution.py:154
  31.4 2.9 %collective-permute-start.4 = (bf16[256,256]{1,0:T(8,128)(2,1)S(1)}, bf16[256,256]{1,0:T(8,128)(2,1)S(1)}, u32[]{:S(2)}, u32[]{:S(2)}) collective-permute-start(bf16[256,256]{1,0:T(8,128)(2,1)S(1)} %get-tuple-element.56), channel_id=1, source_target_pairs={{16,0},{24,8},{32,16},{40,24},{48,32},{56,40},{64,48},{72,56},{80,... | collective-permute-start | bytes 393224 | tf_op jit(solution)/shard_map/ppermute | solution.py:36
  34.3 0.8 %shard_map.89 = (bf16[256,2048]{1,0:T(8,128)(2,1)S(1)}, bf16[256,2048]{1,0:T(8,128)(2,1)S(1)}, bf16[256,256]{1,0:T(8,128)(2,1)S(1)}) custom-call(bf16[128,2048]{1,0:T(8,128)(2,1)S(1)} %get-tuple-element.35.qs_ref, bf16[128,2048]{1,0:T(8,128)(2,1)S(1)} %get-tuple-element.36.dos_ref, f32[256,2048]{1,0:T(8,128)S(1)} %get-tuple-element.38.e_ref, ...), custom_call_target="tpu_custom_call" | custom-call | flops 268435456 | bytes 7536640 | tf_op jit(solution)/shard_map/pallas_call | solution.py:154
  35.1 3.9 %collective-permute-start.3 = (bf16[256,256]{1,0:T(8,128)(2,1)S(1)}, bf16[256,256]{1,0:T(8,128)(2,1)S(1)}, u32[]{:S(2)}, u32[]{:S(2)}) collective-permute-start(bf16[256,256]{1,0:T(8,128)(2,1)S(1)} %get-tuple-element.55), channel_id=1, source_target_pairs={{32,0},{40,8},{48,16},{56,24},{64,32},{72,40},{80,48},{88,56},{96,... | collective-permute-start | bytes 393224 | tf_op jit(solution)/shard_map/ppermute | solution.py:36
  39.1 0.8 %shard_map.91 = (bf16[256,2048]{1,0:T(8,128)(2,1)S(1)}, bf16[256,2048]{1,0:T(8,128)(2,1)S(1)}, f32[256,256]{1,0:T(8,128)S(1)}) custom-call(bf16[128,2048]{1,0:T(8,128)(2,1)S(1)} %get-tuple-element.35.qs_ref, bf16[128,2048]{1,0:T(8,128)(2,1)S(1)} %get-tuple-element.36.dos_ref, f32[256,2048]{1,0:T(8,128)S(1)} %get-tuple-element.47.e_ref, ...), custom_call_target="tpu_custom_call" | custom-call | flops 268435456 | bytes 7667712 | tf_op jit(solution)/shard_map/pallas_call | solution.py:154
  39.9 2.1 %shard_map.92 = (bf16[128,2048]{1,0:T(8,128)(2,1)}, bf16[128,2048]{1,0:T(8,128)(2,1)}) custom-call(bf16[256,256]{1,0:T(8,128)(2,1)S(1)} %collective-permute-done.1.kv_ref.far_ref, bf16[256,256]{1,0:T(8,128)(2,1)S(1)} %collective-permute-done.2.kv_ref.mid_ref, bf16[256,256]{1,0:T(8,128)(2,1)S(1)} %pad_maximum_fusion.kv_ref.near_ref, ...), custom_call_target="tpu_custom_call" | custom-call | flops 805306368 | bytes 7733248 | tf_op jit(solution)/shard_map/pallas_call | solution.py:154
  42.0 0.0 collective-permute-done.4
  42.0 0.0 collective-permute-done.3
  42.0 4.6 %collective-permute-start.5 = (bf16[128,256]{1,0:T(8,128)(2,1)S(1)}, bf16[128,256]{1,0:T(8,128)(2,1)S(1)}, u32[]{:S(2)}, u32[]{:S(2)}) collective-permute-start(bf16[128,256]{1,0:T(8,128)(2,1)S(1)} %slice.25), channel_id=1, source_target_pairs={{8,0},{16,8},{24,16},{32,24},{40,32},{48,40},{56,48},{64,56},{72,6... | collective-permute-start | bytes 196616 | tf_op jit(solution)/shard_map/ppermute | solution.py:36
  46.7 1.3 %collective-permute-done.5 = bf16[128,256]{1,0:T(8,128)(2,1)S(1)} collective-permute-done((bf16[128,256]{1,0:T(8,128)(2,1)S(1)}, bf16[128,256]{1,0:T(8,128)(2,1)S(1)}, u32[]{:S(2)}, u32[]{:S(2)}) %collective-permute-start.5) | collective-permute-done | bytes 65568 | tf_op jit(solution)/shard_map/ppermute | solution.py:36
  48.0 0.6 %fusion.1 = (bf16[128,128]{1,0:T(8,128)(2,1)}, bf16[128,128]{1,0:T(8,128)(2,1)}) fusion(bf16[128,256]{1,0:T(8,128)(2,1)S(1)} %fusion), kind=kLoop, calls=%fused_computation.5 | loop fusion | bytes 131072 | tf_op jit(solution)/shard_map/slice | solution.py:261
  (4 shorter events, 0.1 us)
Async XLA Ops:
  1.4 16.2 %collective-permute-start = (bf16[128,256]{1,0:T(8,128)(2,1)S(1)}, bf16[128,256]{1,0:T(8,128)(2,1)S(1)}, u32[]{:S(2)}, u32[]{:S(2)}) collective-permute-start(bf16[128,256]{1,0:T(8,128)(2,1)S(1)} %shard_map.84), channel_id=1, source_target_pairs={{0,8},{8,16},{16,24},{24,32},{32,40},{40,48},{48,56},{56,64},{64,7... | collective-permute-start | bytes 196616 | tf_op jit(solution)/shard_map/ppermute | solution.py:36
  17.6 7.5 %collective-permute-start.1 = (bf16[256,256]{1,0:T(8,128)(2,1)S(1)}, bf16[256,256]{1,0:T(8,128)(2,1)S(1)}, u32[]{:S(2)}, u32[]{:S(2)}) collective-permute-start(bf16[256,256]{1,0:T(8,128)(2,1)S(1)} %pad_maximum_fusion.kv_ref.near_ref), channel_id=1, source_target_pairs={{0,32},{8,40},{16,48},{24,56},{32,64},{40,72},{48,80},{56,88},{64,... | collective-permute-start | bytes 393224 | tf_op jit(solution)/shard_map/ppermute | solution.py:36
  19.6 9.9 %collective-permute-start.2 = (bf16[256,256]{1,0:T(8,128)(2,1)S(1)}, bf16[256,256]{1,0:T(8,128)(2,1)S(1)}, u32[]{:S(2)}, u32[]{:S(2)}) collective-permute-start(bf16[256,256]{1,0:T(8,128)(2,1)S(1)} %pad_maximum_fusion.kv_ref.near_ref), channel_id=1, source_target_pairs={{0,16},{8,24},{16,32},{24,40},{32,48},{40,56},{48,64},{56,72},{64,... | collective-permute-start | bytes 393224 | tf_op jit(solution)/shard_map/ppermute | solution.py:36
  31.4 10.6 %collective-permute-start.4 = (bf16[256,256]{1,0:T(8,128)(2,1)S(1)}, bf16[256,256]{1,0:T(8,128)(2,1)S(1)}, u32[]{:S(2)}, u32[]{:S(2)}) collective-permute-start(bf16[256,256]{1,0:T(8,128)(2,1)S(1)} %get-tuple-element.56), channel_id=1, source_target_pairs={{16,0},{24,8},{32,16},{40,24},{48,32},{56,40},{64,48},{72,56},{80,... | collective-permute-start | bytes 393224 | tf_op jit(solution)/shard_map/ppermute | solution.py:36
  35.1 6.8 %collective-permute-start.3 = (bf16[256,256]{1,0:T(8,128)(2,1)S(1)}, bf16[256,256]{1,0:T(8,128)(2,1)S(1)}, u32[]{:S(2)}, u32[]{:S(2)}) collective-permute-start(bf16[256,256]{1,0:T(8,128)(2,1)S(1)} %get-tuple-element.55), channel_id=1, source_target_pairs={{32,0},{40,8},{48,16},{56,24},{64,32},{72,40},{80,48},{88,56},{96,... | collective-permute-start | bytes 393224 | tf_op jit(solution)/shard_map/ppermute | solution.py:36
  42.0 5.9 %collective-permute-start.5 = (bf16[128,256]{1,0:T(8,128)(2,1)S(1)}, bf16[128,256]{1,0:T(8,128)(2,1)S(1)}, u32[]{:S(2)}, u32[]{:S(2)}) collective-permute-start(bf16[128,256]{1,0:T(8,128)(2,1)S(1)} %slice.25), channel_id=1, source_target_pairs={{8,0},{16,8},{24,16},{32,24},{40,32},{48,40},{56,48},{64,56},{72,6... | collective-permute-start | bytes 196616 | tf_op jit(solution)/shard_map/ppermute | solution.py:36

commit v5 on v4

--- a/solution.py
+++ b/solution.py
@@ -237,7 +237,6 @@
     own = join(keys, values)
     before = shifted(own, 1)
     qs, dos, bias = prepare(doc_lens, index, queries, output_gradient)
-    before, bias = lax.optimization_barrier((before, bias))
     near = jnp.concatenate([before, own], 0)
     mid = shifted(near, 2)
     far = shifted(near, 4)

time: 49 us -> 49 us (level)
  no operation moved by 1% of the time
where the time goes in v5:
time: 49 us; the launch traced here: 48.6 us
  starting transfers between devices  19.3 us (39%)
  waiting for transfers between devices  18.2 us (37%)
  Pallas kernels  9.74 us (20%)
  between operations  0.76 us (2%)
  local copies, waits for them, and re-layouts  0.64 us (1%)
    ppermute x6, starting transfers between devices, shifted(): return lax.ppermute(block, SEQ_AXES, route)  19.3 us
    ppermute x6, waiting for transfers between devices, shifted(): return lax.ppermute(block, SEQ_AXES, route)  18.2 us
    pallas_call x9, Pallas kernels, call(): pl.pallas_call(kernel, out_shape=outs, in_specs=specs, out_specs=(vmem,)...  9.74 us
  transfers between devices with their start and end apart: 6, of which 4 were waited for; matrix products, arithmetic and copies ran while one was open for 0% of the time, Pallas kernels for 15%

profile of v5, /device:TPU:1, one launch (start us, length us, event | category | flops | bytes accessed | tf_op | source)
XLA Modules:
  0.0 48.6 jit_solution(2542662216193309232)
XLA Ops:
  0.6 0.8 %shard_map.84 = bf16[128,256]{1,0:T(8,128)(2,1)S(1)} custom-call(bf16[128,128]{1,0:T(8,128)(2,1)} %k_ref.1, bf16[128,128]{1,0:T(8,128)(2,1)} %v_ref.1), custom_call_target="tpu_custom_call" | custom-call | bytes 131072 | tf_op jit(solution)/shard_map/pallas_call | solution.py:154
  1.4 3.9 %collective-permute-start = (bf16[128,256]{1,0:T(8,128)(2,1)S(1)}, bf16[128,256]{1,0:T(8,128)(2,1)S(1)}, u32[]{:S(2)}, u32[]{:S(2)}) collective-permute-start(bf16[128,256]{1,0:T(8,128)(2,1)S(1)} %shard_map.84), channel_id=1, source_target_pairs={{0,8},{8,16},{16,24},{24,32},{32,40},{40,48},{48,56},{56,64},{64,7... | collective-permute-start | bytes 196616 | tf_op jit(solution)/shard_map/ppermute | solution.py:36
  5.4 12.2 %collective-permute-done = bf16[128,256]{1,0:T(8,128)(2,1)S(1)} collective-permute-done((bf16[128,256]{1,0:T(8,128)(2,1)S(1)}, bf16[128,256]{1,0:T(8,128)(2,1)S(1)}, u32[]{:S(2)}, u32[]{:S(2)}) %collective-permute-start) | collective-permute-done | bytes 65568 | tf_op jit(solution)/shard_map/ppermute | solution.py:36
  17.6 1.9 %collective-permute-start.1 = (bf16[256,256]{1,0:T(8,128)(2,1)S(1)}, bf16[256,256]{1,0:T(8,128)(2,1)S(1)}, u32[]{:S(2)}, u32[]{:S(2)}) collective-permute-start(bf16[256,256]{1,0:T(8,128)(2,1)S(1)} %pad_maximum_fusion.kv_ref.near_ref), channel_id=1, source_target_pairs={{0,32},{8,40},{16,48},{24,56},{32,64},{40,72},{48,80},{56,88},{64,... | collective-permute-start | bytes 393224 | tf_op jit(solution)/shard_map/ppermute | solution.py:36
  19.6 1.9 %collective-permute-start.2 = (bf16[256,256]{1,0:T(8,128)(2,1)S(1)}, bf16[256,256]{1,0:T(8,128)(2,1)S(1)}, u32[]{:S(2)}, u32[]{:S(2)}) collective-permute-start(bf16[256,256]{1,0:T(8,128)(2,1)S(1)} %pad_maximum_fusion.kv_ref.near_ref), channel_id=1, source_target_pairs={{0,16},{8,24},{16,32},{24,40},{32,48},{40,56},{48,64},{56,72},{64,... | collective-permute-start | bytes 393224 | tf_op jit(solution)/shard_map/ppermute | solution.py:36
  21.5 1.4 %shard_map.85 = (bf16[128,2048]{1,0:T(8,128)(2,1)S(1)}, bf16[128,2048]{1,0:T(8,128)(2,1)S(1)}, f32[768,128]{1,0:T(8,128)S(1)}) custom-call(s32[32]{0:T(128)} %lens_hbm.1, s32[1]{0:T(128)} %bitcast.index_ref, bf16[128,2048]{1,0:T(8,128)(2,1)} %q_hbm.1, bf16[128,2048]{1,0:T(8,128)(2,1)} %do_hbm.1), custom_call_target="tpu_custom_call" | custom-call | bytes 2490500 | tf_op jit(solution)/shard_map/pallas_call | solution.py:154
  22.9 1.0 %shard_map.87 = (f32[256,2048]{1,0:T(8,128)S(1)}, f32[256,2048]{1,0:T(8,128)S(1)}, f32[8,2048]{1,0:T(8,128)S(1)}) custom-call(bf16[128,2048]{1,0:T(8,128)(2,1)S(1)} %get-tuple-element.31.qs_ref, bf16[128,2048]{1,0:T(8,128)(2,1)S(1)} %get-tuple-element.32.dos_ref, bf16[256,256]{1,0:T(8,128)(2,1)S(1)} %pad_maximum_fusion.kv_ref.near_ref, ...), custom_call_target="tpu_custom_call" | custom-call | flops 268435456 | bytes 5832704 | tf_op jit(solution)/shard_map/pallas_call | solution.py:154
  23.9 1.3 %collective-permute-done.1.kv_ref.far_ref = bf16[256,256]{1,0:T(8,128)(2,1)S(1)} collective-permute-done((bf16[256,256]{1,0:T(8,128)(2,1)S(1)}, bf16[256,256]{1,0:T(8,128)(2,1)S(1)}, u32[]{:S(2)}, u32[]{:S(2)}) %collective-permute-start.1) | collective-permute-done | bytes 131104 | tf_op jit(solution)/shard_map/ppermute | solution.py:36
  25.1 1.0 %shard_map.86 = (f32[256,2048]{1,0:T(8,128)S(1)}, f32[256,2048]{1,0:T(8,128)S(1)}, f32[8,2048]{1,0:T(8,128)S(1)}) custom-call(bf16[128,2048]{1,0:T(8,128)(2,1)S(1)} %get-tuple-element.31.qs_ref, bf16[128,2048]{1,0:T(8,128)(2,1)S(1)} %get-tuple-element.32.dos_ref, bf16[256,256]{1,0:T(8,128)(2,1)S(1)} %collective-permute-done.1.kv_ref.far_ref, ...), custom_call_target="tpu_custom_call" | custom-call | flops 268435456 | bytes 5832704 | tf_op jit(solution)/shard_map/pallas_call | solution.py:154
  26.1 3.3 %collective-permute-done.2.kv_ref.mid_ref = bf16[256,256]{1,0:T(8,128)(2,1)S(1)} collective-permute-done((bf16[256,256]{1,0:T(8,128)(2,1)S(1)}, bf16[256,256]{1,0:T(8,128)(2,1)S(1)}, u32[]{:S(2)}, u32[]{:S(2)}) %collective-permute-start.2) | collective-permute-done | bytes 131104 | tf_op jit(solution)/shard_map/ppermute | solution.py:36
  29.5 1.0 %shard_map.88 = (f32[256,2048]{1,0:T(8,128)S(1)}, f32[256,2048]{1,0:T(8,128)S(1)}, f32[8,2048]{1,0:T(8,128)S(1)}) custom-call(bf16[128,2048]{1,0:T(8,128)(2,1)S(1)} %get-tuple-element.31.qs_ref, bf16[128,2048]{1,0:T(8,128)(2,1)S(1)} %get-tuple-element.32.dos_ref, bf16[256,256]{1,0:T(8,128)(2,1)S(1)} %collective-permute-done.2.kv_ref.mid_ref, ...), custom_call_target="tpu_custom_call" | custom-call | flops 268435456 | bytes 5963776 | tf_op jit(solution)/shard_map/pallas_call | solution.py:154
  30.5 0.8 %shard_map.90 = (bf16[256,2048]{1,0:T(8,128)(2,1)S(1)}, bf16[256,2048]{1,0:T(8,128)(2,1)S(1)}, bf16[256,256]{1,0:T(8,128)(2,1)S(1)}) custom-call(bf16[128,2048]{1,0:T(8,128)(2,1)S(1)} %get-tuple-element.31.qs_ref, bf16[128,2048]{1,0:T(8,128)(2,1)S(1)} %get-tuple-element.32.dos_ref, f32[256,2048]{1,0:T(8,128)S(1)} %get-tuple-element.40.e_ref, ...), custom_call_target="tpu_custom_call" | custom-call | flops 268435456 | bytes 7536640 | tf_op jit(solution)/shard_map/pallas_call | solution.py:154
  31.4 2.9 %collective-permute-start.4 = (bf16[256,256]{1,0:T(8,128)(2,1)S(1)}, bf16[256,256]{1,0:T(8,128)(2,1)S(1)}, u32[]{:S(2)}, u32[]{:S(2)}) collective-permute-start(bf16[256,256]{1,0:T(8,128)(2,1)S(1)} %get-tuple-element.52), channel_id=1, source_target_pairs={{16,0},{24,8},{32,16},{40,24},{48,32},{56,40},{64,48},{72,56},{80,... | collective-permute-start | bytes 393224 | tf_op jit(solution)/shard_map/ppermute | solution.py:36
  34.3 0.8 %shard_map.89 = (bf16[256,2048]{1,0:T(8,128)(2,1)S(1)}, bf16[256,2048]{1,0:T(8,128)(2,1)S(1)}, bf16[256,256]{1,0:T(8,128)(2,1)S(1)}) custom-call(bf16[128,2048]{1,0:T(8,128)(2,1)S(1)} %get-tuple-element.31.qs_ref, bf16[128,2048]{1,0:T(8,128)(2,1)S(1)} %get-tuple-element.32.dos_ref, f32[256,2048]{1,0:T(8,128)S(1)} %get-tuple-element.34.e_ref, ...), custom_call_target="tpu_custom_call" | custom-call | flops 268435456 | bytes 7536640 | tf_op jit(solution)/shard_map/pallas_call | solution.py:154
  35.1 3.9 %collective-permute-start.3 = (bf16[256,256]{1,0:T(8,128)(2,1)S(1)}, bf16[256,256]{1,0:T(8,128)(2,1)S(1)}, u32[]{:S(2)}, u32[]{:S(2)}) collective-permute-start(bf16[256,256]{1,0:T(8,128)(2,1)S(1)} %get-tuple-element.51), channel_id=1, source_target_pairs={{32,0},{40,8},{48,16},{56,24},{64,32},{72,40},{80,48},{88,56},{96,... | collective-permute-start | bytes 393224 | tf_op jit(solution)/shard_map/ppermute | solution.py:36
  39.1 0.8 %shard_map.91 = (bf16[256,2048]{1,0:T(8,128)(2,1)S(1)}, bf16[256,2048]{1,0:T(8,128)(2,1)S(1)}, f32[256,256]{1,0:T(8,128)S(1)}) custom-call(bf16[128,2048]{1,0:T(8,128)(2,1)S(1)} %get-tuple-element.31.qs_ref, bf16[128,2048]{1,0:T(8,128)(2,1)S(1)} %get-tuple-element.32.dos_ref, f32[256,2048]{1,0:T(8,128)S(1)} %get-tuple-element.43.e_ref, ...), custom_call_target="tpu_custom_call" | custom-call | flops 268435456 | bytes 7667712 | tf_op jit(solution)/shard_map/pallas_call | solution.py:154
  39.9 2.1 %shard_map.92 = (bf16[128,2048]{1,0:T(8,128)(2,1)}, bf16[128,2048]{1,0:T(8,128)(2,1)}) custom-call(bf16[256,256]{1,0:T(8,128)(2,1)S(1)} %collective-permute-done.1.kv_ref.far_ref, bf16[256,256]{1,0:T(8,128)(2,1)S(1)} %collective-permute-done.2.kv_ref.mid_ref, bf16[256,256]{1,0:T(8,128)(2,1)S(1)} %pad_maximum_fusion.kv_ref.near_ref, ...), custom_call_target="tpu_custom_call" | custom-call | flops 805306368 | bytes 7733248 | tf_op jit(solution)/shard_map/pallas_call | solution.py:154
  42.0 0.0 collective-permute-done.4
  42.0 0.0 collective-permute-done.3
  42.0 4.6 %collective-permute-start.5 = (bf16[128,256]{1,0:T(8,128)(2,1)S(1)}, bf16[128,256]{1,0:T(8,128)(2,1)S(1)}, u32[]{:S(2)}, u32[]{:S(2)}) collective-permute-start(bf16[128,256]{1,0:T(8,128)(2,1)S(1)} %slice.25), channel_id=1, source_target_pairs={{8,0},{16,8},{24,16},{32,24},{40,32},{48,40},{56,48},{64,56},{72,6... | collective-permute-start | bytes 196616 | tf_op jit(solution)/shard_map/ppermute | solution.py:36
  46.7 1.3 %collective-permute-done.5 = bf16[128,256]{1,0:T(8,128)(2,1)S(1)} collective-permute-done((bf16[128,256]{1,0:T(8,128)(2,1)S(1)}, bf16[128,256]{1,0:T(8,128)(2,1)S(1)}, u32[]{:S(2)}, u32[]{:S(2)}) %collective-permute-start.5) | collective-permute-done | bytes 65568 | tf_op jit(solution)/shard_map/ppermute | solution.py:36
  48.0 0.6 %fusion.1 = (bf16[128,128]{1,0:T(8,128)(2,1)}, bf16[128,128]{1,0:T(8,128)(2,1)}) fusion(bf16[128,256]{1,0:T(8,128)(2,1)S(1)} %fusion), kind=kLoop, calls=%fused_computation.5 | loop fusion | bytes 131072 | tf_op jit(solution)/shard_map/slice | solution.py:260
  (4 shorter events, 0.1 us)
Async XLA Ops:
  1.4 16.2 %collective-permute-start = (bf16[128,256]{1,0:T(8,128)(2,1)S(1)}, bf16[128,256]{1,0:T(8,128)(2,1)S(1)}, u32[]{:S(2)}, u32[]{:S(2)}) collective-permute-start(bf16[128,256]{1,0:T(8,128)(2,1)S(1)} %shard_map.84), channel_id=1, source_target_pairs={{0,8},{8,16},{16,24},{24,32},{32,40},{40,48},{48,56},{56,64},{64,7... | collective-permute-start | bytes 196616 | tf_op jit(solution)/shard_map/ppermute | solution.py:36
  17.6 7.5 %collective-permute-start.1 = (bf16[256,256]{1,0:T(8,128)(2,1)S(1)}, bf16[256,256]{1,0:T(8,128)(2,1)S(1)}, u32[]{:S(2)}, u32[]{:S(2)}) collective-permute-start(bf16[256,256]{1,0:T(8,128)(2,1)S(1)} %pad_maximum_fusion.kv_ref.near_ref), channel_id=1, source_target_pairs={{0,32},{8,40},{16,48},{24,56},{32,64},{40,72},{48,80},{56,88},{64,... | collective-permute-start | bytes 393224 | tf_op jit(solution)/shard_map/ppermute | solution.py:36
  19.6 9.9 %collective-permute-start.2 = (bf16[256,256]{1,0:T(8,128)(2,1)S(1)}, bf16[256,256]{1,0:T(8,128)(2,1)S(1)}, u32[]{:S(2)}, u32[]{:S(2)}) collective-permute-start(bf16[256,256]{1,0:T(8,128)(2,1)S(1)} %pad_maximum_fusion.kv_ref.near_ref), channel_id=1, source_target_pairs={{0,16},{8,24},{16,32},{24,40},{32,48},{40,56},{48,64},{56,72},{64,... | collective-permute-start | bytes 393224 | tf_op jit(solution)/shard_map/ppermute | solution.py:36
  31.4 10.6 %collective-permute-start.4 = (bf16[256,256]{1,0:T(8,128)(2,1)S(1)}, bf16[256,256]{1,0:T(8,128)(2,1)S(1)}, u32[]{:S(2)}, u32[]{:S(2)}) collective-permute-start(bf16[256,256]{1,0:T(8,128)(2,1)S(1)} %get-tuple-element.52), channel_id=1, source_target_pairs={{16,0},{24,8},{32,16},{40,24},{48,32},{56,40},{64,48},{72,56},{80,... | collective-permute-start | bytes 393224 | tf_op jit(solution)/shard_map/ppermute | solution.py:36
  35.1 6.8 %collective-permute-start.3 = (bf16[256,256]{1,0:T(8,128)(2,1)S(1)}, bf16[256,256]{1,0:T(8,128)(2,1)S(1)}, u32[]{:S(2)}, u32[]{:S(2)}) collective-permute-start(bf16[256,256]{1,0:T(8,128)(2,1)S(1)} %get-tuple-element.51), channel_id=1, source_target_pairs={{32,0},{40,8},{48,16},{56,24},{64,32},{72,40},{80,48},{88,56},{96,... | collective-permute-start | bytes 393224 | tf_op jit(solution)/shard_map/ppermute | solution.py:36
  42.0 5.9 %collective-permute-start.5 = (bf16[128,256]{1,0:T(8,128)(2,1)S(1)}, bf16[128,256]{1,0:T(8,128)(2,1)S(1)}, u32[]{:S(2)}, u32[]{:S(2)}) collective-permute-start(bf16[128,256]{1,0:T(8,128)(2,1)S(1)} %slice.25), channel_id=1, source_target_pairs={{8,0},{16,8},{24,16},{32,24},{40,32},{48,40},{56,48},{64,56},{72,6... | collective-permute-start | bytes 196616 | tf_op jit(solution)/shard_map/ppermute | solution.py:36

commit v6 on v5

--- a/solution.py
+++ b/solution.py
@@ -132,18 +132,15 @@
     grads(qs_ref, dos_ref, w_ref, ds_ref, out_ref)
 
 
-def query_kernel(far_ref, mid_ref, near_ref, *refs):
-    ws, dss, (o_ref, dq_ref, t_ref) = refs[:3], refs[3:6], refs[6:]
+def query_kernel(side, scale, far_ref, mid_ref, near_ref, *refs):
+    ws, (out_ref, t_ref) = refs[:3], refs[3:]
     for t, ref in enumerate((far_ref, mid_ref, near_ref)):
-        t_ref[:, pl.ds(t * CHUNK, CHUNK)] = ref[...].T
+        t_ref[:, pl.ds(t * CHUNK, CHUNK)] = ref[:, side].T
     for j, part in enumerate(pl.ds(j * STEP, STEP) for j in range(ws[0].shape[1] // STEP)):
         w = jnp.concatenate([ref[:, part] for ref in ws], 0)
-        ds = jnp.concatenate([ref[:, part] for ref in dss], 0)
-        o = dot(t_ref[HEAD:, :], w, NN).astype(BF16)
-        dq = (dot(t_ref[:HEAD, :], ds, NN) * SCALE).astype(BF16)
-        for x, ref in ((o, o_ref), (dq, dq_ref)):
-            ref[:, pl.ds(j * STEP, HEAD)] = x[:, :TILE].T
-            ref[:, pl.ds(j * STEP + HEAD, HEAD)] = x[:, TILE:].T
+        x = (dot(t_ref[...], w, NN) * scale).astype(BF16)
+        out_ref[:, pl.ds(j * STEP, HEAD)] = x[:, :TILE].T
+        out_ref[:, pl.ds(j * STEP + HEAD, HEAD)] = x[:, TILE:].T
 
 
 def call(kernel, args, outs, flops=0, scratch=(), spaces=None, limit=16):
@@ -224,12 +221,12 @@
     )
 
 
-def query_part(kvs, ws, dss, shape):
+def query_part(side, scale, kvs, ws, shape):
     n = ws[0].shape[1]
     return call(
-        query_kernel, (*kvs, *ws, *dss), ((shape, BF16), (shape, BF16)),
-        4 * SPAN * n * HEAD, scratch=(pltpu.VMEM((2 * HEAD, SPAN), BF16),),
-    )
+        functools.partial(query_kernel, side, scale), (*kvs, *ws), ((shape, BF16),),
+        2 * SPAN * n * HEAD, scratch=(pltpu.VMEM((HEAD, SPAN), BF16),),
+    )[0]
 
 
 def per_device(queries, keys, values, output_gradient, doc_lens):
@@ -248,14 +245,12 @@
     w_far, ds_far, g_far = grad_part(1, qs, dos, e_far, dp_far, stats, BF16)
     from_far = shifted(g_far, -4)
     w_near, ds_near, g_near = grad_part(0, qs, dos, e_near, dp_near, stats, F32)
-    attended, query_grad = query_part(
-        (far, mid, near), (w_far, w_mid, w_near), (ds_far, ds_mid, ds_near), queries.shape
-    )
-    attended, query_grad, from_far, from_mid = lax.optimization_barrier(
-        (attended, query_grad, from_far, from_mid)
-    )
+    kvs = (far, mid, near)
+    attended = query_part(VALUE, 1.0, kvs, (w_far, w_mid, w_near), queries.shape)
+    attended, from_far, from_mid = lax.optimization_barrier((attended, from_far, from_mid))
     summed = from_far.astype(F32) + from_mid.astype(F32) + g_near
     back = shifted(summed[:TILE].astype(BF16), -1).astype(F32)
+    query_grad = query_part(KEY, SCALE, kvs, (ds_far, ds_mid, ds_near), queries.shape)
     total = (summed[TILE:] + back).astype(BF16)
     return attended, query_grad, total[:, :HEAD], total[:, HEAD:]
 

time: 49 us -> 49.1 us (level)
  waiting for transfers between devices: 18.2 us -> 16.9 us
  Pallas kernels: 9.74 us -> 10.6 us
  starting transfers between devices: 19.3 us -> 19.9 us
    ppermute x6, waiting for transfers between devices: 18.2 us -> 16.9 us  [shifted(): return lax.ppermute(block, SEQ_AXES, route)]
    pallas_call x9 -> x10, Pallas kernels: 9.74 us -> 10.6 us  [call(): pl.pallas_call(kernel, out_shape=outs, in_specs=specs, out_specs=(vmem,)...]
    ppermute x6, starting transfers between devices: 19.3 us -> 19.9 us  [shifted(): return lax.ppermute(block, SEQ_AXES, route)]
  transfers between devices with their start and end apart: 6 -> 6, of which waited for: 4 -> 3; matrix products, arithmetic and copies ran while one was open for 0% -> 0% of each run, Pallas kernels for 15% -> 16%
where the time goes in v6:
time: 49.1 us; the launch traced here: 48.8 us
  starting transfers between devices  19.9 us (41%)
  waiting for transfers between devices  16.9 us (34%)
  Pallas kernels  10.6 us (22%)
  between operations  0.76 us (2%)
  local copies, waits for them, and re-layouts  0.64 us (1%)
    ppermute x6, starting transfers between devices, shifted(): return lax.ppermute(block, SEQ_AXES, route)  19.9 us
    ppermute x6, waiting for transfers between devices, shifted(): return lax.ppermute(block, SEQ_AXES, route)  16.9 us
    pallas_call x10, Pallas kernels, call(): pl.pallas_call(kernel, out_shape=outs, in_specs=specs, out_specs=(vmem,)...  10.6 us
  transfers between devices with their start and end apart: 6, of which 3 were waited for; matrix products, arithmetic and copies ran while one was open for 0% of the time, Pallas kernels for 16%

profile of v6, /device:TPU:1, one launch (start us, length us, event | category | flops | bytes accessed | tf_op | source)
XLA Modules:
  0.0 48.8 jit_solution(2157608609900118536)
XLA Ops:
  0.6 0.8 %shard_map.84 = bf16[128,256]{1,0:T(8,128)(2,1)S(1)} custom-call(bf16[128,128]{1,0:T(8,128)(2,1)} %k_ref.1, bf16[128,128]{1,0:T(8,128)(2,1)} %v_ref.1), custom_call_target="tpu_custom_call" | custom-call | bytes 131072 | tf_op jit(solution)/shard_map/pallas_call | solution.py:151
  1.4 3.9 %collective-permute-start = (bf16[128,256]{1,0:T(8,128)(2,1)S(1)}, bf16[128,256]{1,0:T(8,128)(2,1)S(1)}, u32[]{:S(2)}, u32[]{:S(2)}) collective-permute-start(bf16[128,256]{1,0:T(8,128)(2,1)S(1)} %shard_map.84), channel_id=1, source_target_pairs={{0,8},{8,16},{16,24},{24,32},{32,40},{40,48},{48,56},{56,64},{64,7... | collective-permute-start | bytes 196616 | tf_op jit(solution)/shard_map/ppermute | solution.py:36
  5.4 12.2 %collective-permute-done = bf16[128,256]{1,0:T(8,128)(2,1)S(1)} collective-permute-done((bf16[128,256]{1,0:T(8,128)(2,1)S(1)}, bf16[128,256]{1,0:T(8,128)(2,1)S(1)}, u32[]{:S(2)}, u32[]{:S(2)}) %collective-permute-start) | collective-permute-done | bytes 65568 | tf_op jit(solution)/shard_map/ppermute | solution.py:36
  17.6 1.9 %collective-permute-start.1 = (bf16[256,256]{1,0:T(8,128)(2,1)S(1)}, bf16[256,256]{1,0:T(8,128)(2,1)S(1)}, u32[]{:S(2)}, u32[]{:S(2)}) collective-permute-start(bf16[256,256]{1,0:T(8,128)(2,1)S(1)} %pad_maximum_fusion.kv_ref.near_ref), channel_id=1, source_target_pairs={{0,32},{8,40},{16,48},{24,56},{32,64},{40,72},{48,80},{56,88},{64,... | collective-permute-start | bytes 393224 | tf_op jit(solution)/shard_map/ppermute | solution.py:36
  19.6 1.9 %collective-permute-start.2 = (bf16[256,256]{1,0:T(8,128)(2,1)S(1)}, bf16[256,256]{1,0:T(8,128)(2,1)S(1)}, u32[]{:S(2)}, u32[]{:S(2)}) collective-permute-start(bf16[256,256]{1,0:T(8,128)(2,1)S(1)} %pad_maximum_fusion.kv_ref.near_ref), channel_id=1, source_target_pairs={{0,16},{8,24},{16,32},{24,40},{32,48},{40,56},{48,64},{56,72},{64,... | collective-permute-start | bytes 393224 | tf_op jit(solution)/shard_map/ppermute | solution.py:36
  21.5 1.4 %shard_map.85 = (bf16[128,2048]{1,0:T(8,128)(2,1)S(1)}, bf16[128,2048]{1,0:T(8,128)(2,1)S(1)}, f32[768,128]{1,0:T(8,128)S(1)}) custom-call(s32[32]{0:T(128)} %lens_hbm.1, s32[1]{0:T(128)} %bitcast.index_ref, bf16[128,2048]{1,0:T(8,128)(2,1)} %q_hbm.1, bf16[128,2048]{1,0:T(8,128)(2,1)} %do_hbm.1), custom_call_target="tpu_custom_call" | custom-call | bytes 2490500 | tf_op jit(solution)/shard_map/pallas_call | solution.py:151
  22.9 1.0 %shard_map.87 = (f32[256,2048]{1,0:T(8,128)S(1)}, f32[256,2048]{1,0:T(8,128)S(1)}, f32[8,2048]{1,0:T(8,128)S(1)}) custom-call(bf16[128,2048]{1,0:T(8,128)(2,1)S(1)} %get-tuple-element.28.qs_ref, bf16[128,2048]{1,0:T(8,128)(2,1)S(1)} %get-tuple-element.29.dos_ref, bf16[256,256]{1,0:T(8,128)(2,1)S(1)} %pad_maximum_fusion.kv_ref.near_ref, ...), custom_call_target="tpu_custom_call" | custom-call | flops 268435456 | bytes 5832704 | tf_op jit(solution)/shard_map/pallas_call | solution.py:151
  23.9 1.3 %collective-permute-done.1.kv_ref.far_ref = bf16[256,256]{1,0:T(8,128)(2,1)S(1)} collective-permute-done((bf16[256,256]{1,0:T(8,128)(2,1)S(1)}, bf16[256,256]{1,0:T(8,128)(2,1)S(1)}, u32[]{:S(2)}, u32[]{:S(2)}) %collective-permute-start.1) | collective-permute-done | bytes 131104 | tf_op jit(solution)/shard_map/ppermute | solution.py:36
  25.1 1.0 %shard_map.86 = (f32[256,2048]{1,0:T(8,128)S(1)}, f32[256,2048]{1,0:T(8,128)S(1)}, f32[8,2048]{1,0:T(8,128)S(1)}) custom-call(bf16[128,2048]{1,0:T(8,128)(2,1)S(1)} %get-tuple-element.28.qs_ref, bf16[128,2048]{1,0:T(8,128)(2,1)S(1)} %get-tuple-element.29.dos_ref, bf16[256,256]{1,0:T(8,128)(2,1)S(1)} %collective-permute-done.1.kv_ref.far_ref, ...), custom_call_target="tpu_custom_call" | custom-call | flops 268435456 | bytes 5832704 | tf_op jit(solution)/shard_map/pallas_call | solution.py:151
  26.1 3.3 %collective-permute-done.2.kv_ref.mid_ref = bf16[256,256]{1,0:T(8,128)(2,1)S(1)} collective-permute-done((bf16[256,256]{1,0:T(8,128)(2,1)S(1)}, bf16[256,256]{1,0:T(8,128)(2,1)S(1)}, u32[]{:S(2)}, u32[]{:S(2)}) %collective-permute-start.2) | collective-permute-done | bytes 131104 | tf_op jit(solution)/shard_map/ppermute | solution.py:36
  29.5 1.0 %shard_map.88 = (f32[256,2048]{1,0:T(8,128)S(1)}, f32[256,2048]{1,0:T(8,128)S(1)}, f32[8,2048]{1,0:T(8,128)S(1)}) custom-call(bf16[128,2048]{1,0:T(8,128)(2,1)S(1)} %get-tuple-element.28.qs_ref, bf16[128,2048]{1,0:T(8,128)(2,1)S(1)} %get-tuple-element.29.dos_ref, bf16[256,256]{1,0:T(8,128)(2,1)S(1)} %collective-permute-done.2.kv_ref.mid_ref, ...), custom_call_target="tpu_custom_call" | custom-call | flops 268435456 | bytes 5963776 | tf_op jit(solution)/shard_map/pallas_call | solution.py:151
  30.5 0.8 %shard_map.90 = (bf16[256,2048]{1,0:T(8,128)(2,1)S(1)}, bf16[256,2048]{1,0:T(8,128)(2,1)S(1)}, bf16[256,256]{1,0:T(8,128)(2,1)S(1)}) custom-call(bf16[128,2048]{1,0:T(8,128)(2,1)S(1)} %get-tuple-element.28.qs_ref, bf16[128,2048]{1,0:T(8,128)(2,1)S(1)} %get-tuple-element.29.dos_ref, f32[256,2048]{1,0:T(8,128)S(1)} %get-tuple-element.37.e_ref, ...), custom_call_target="tpu_custom_call" | custom-call | flops 268435456 | bytes 7536640 | tf_op jit(solution)/shard_map/pallas_call | solution.py:151
  31.4 2.9 %collective-permute-start.4 = (bf16[256,256]{1,0:T(8,128)(2,1)S(1)}, bf16[256,256]{1,0:T(8,128)(2,1)S(1)}, u32[]{:S(2)}, u32[]{:S(2)}) collective-permute-start(bf16[256,256]{1,0:T(8,128)(2,1)S(1)} %get-tuple-element.44), channel_id=1, source_target_pairs={{16,0},{24,8},{32,16},{40,24},{48,32},{56,40},{64,48},{72,56},{80,... | collective-permute-start | bytes 393224 | tf_op jit(solution)/shard_map/ppermute | solution.py:36
  34.3 0.8 %shard_map.89 = (bf16[256,2048]{1,0:T(8,128)(2,1)S(1)}, bf16[256,2048]{1,0:T(8,128)(2,1)S(1)}, bf16[256,256]{1,0:T(8,128)(2,1)S(1)}) custom-call(bf16[128,2048]{1,0:T(8,128)(2,1)S(1)} %get-tuple-element.28.qs_ref, bf16[128,2048]{1,0:T(8,128)(2,1)S(1)} %get-tuple-element.29.dos_ref, f32[256,2048]{1,0:T(8,128)S(1)} %get-tuple-element.31.e_ref, ...), custom_call_target="tpu_custom_call" | custom-call | flops 268435456 | bytes 7536640 | tf_op jit(solution)/shard_map/pallas_call | solution.py:151
  35.1 3.9 %collective-permute-start.3 = (bf16[256,256]{1,0:T(8,128)(2,1)S(1)}, bf16[256,256]{1,0:T(8,128)(2,1)S(1)}, u32[]{:S(2)}, u32[]{:S(2)}) collective-permute-start(bf16[256,256]{1,0:T(8,128)(2,1)S(1)} %get-tuple-element.43), channel_id=1, source_target_pairs={{32,0},{40,8},{48,16},{56,24},{64,32},{72,40},{80,48},{88,56},{96,... | collective-permute-start | bytes 393224 | tf_op jit(solution)/shard_map/ppermute | solution.py:36
  39.1 0.8 %shard_map.91 = (bf16[256,2048]{1,0:T(8,128)(2,1)S(1)}, bf16[256,2048]{1,0:T(8,128)(2,1)S(1)}, f32[256,256]{1,0:T(8,128)S(1)}) custom-call(bf16[128,2048]{1,0:T(8,128)(2,1)S(1)} %get-tuple-element.28.qs_ref, bf16[128,2048]{1,0:T(8,128)(2,1)S(1)} %get-tuple-element.29.dos_ref, f32[256,2048]{1,0:T(8,128)S(1)} %get-tuple-element.40.e_ref, ...), custom_call_target="tpu_custom_call" | custom-call | flops 268435456 | bytes 7667712 | tf_op jit(solution)/shard_map/pallas_call | solution.py:151
  39.9 1.5 %shard_map.92 = bf16[128,2048]{1,0:T(8,128)(2,1)} custom-call(bf16[256,256]{1,0:T(8,128)(2,1)S(1)} %collective-permute-done.1.kv_ref.far_ref, bf16[256,256]{1,0:T(8,128)(2,1)S(1)} %collective-permute-done.2.kv_ref.mid_ref, bf16[256,256]{1,0:T(8,128)(2,1)S(1)} %pad_maximum_fusion.kv_ref.near_ref, bf16[256,2048]{1,0:T(8,128)(2,1)S(1)} %get-tuple-element.36.refs_0_, ...), custom_call_target="tpu_custom_call" | custom-call | flops 402653184 | bytes 4063232 | tf_op jit(solution)/shard_map/pallas_call | solution.py:151
  41.4 0.0 collective-permute-done.4
  41.4 0.0 collective-permute-done.3
  41.5 5.2 %collective-permute-start.5 = (bf16[128,256]{1,0:T(8,128)(2,1)S(1)}, bf16[128,256]{1,0:T(8,128)(2,1)S(1)}, u32[]{:S(2)}, u32[]{:S(2)}) collective-permute-start(bf16[128,256]{1,0:T(8,128)(2,1)S(1)} %slice.25), channel_id=1, source_target_pairs={{8,0},{16,8},{24,16},{32,24},{40,32},{48,40},{56,48},{64,56},{72,6... | collective-permute-start | bytes 196616 | tf_op jit(solution)/shard_map/ppermute | solution.py:36
  46.7 1.5 %shard_map.93 = bf16[128,2048]{1,0:T(8,128)(2,1)} custom-call(bf16[256,256]{1,0:T(8,128)(2,1)S(1)} %collective-permute-done.1.kv_ref.far_ref, bf16[256,256]{1,0:T(8,128)(2,1)S(1)} %collective-permute-done.2.kv_ref.mid_ref, bf16[256,256]{1,0:T(8,128)(2,1)S(1)} %pad_maximum_fusion.kv_ref.near_ref, bf16[256,2048]{1,0:T(8,128)(2,1)S(1)} %get-tuple-element.46.refs_0_, ...), custom_call_target="tpu_custom_call" | custom-call | flops 402653184 | bytes 4063232 | tf_op jit(solution)/shard_map/pallas_call | solution.py:151
  48.1 0.0 collective-permute-done.5
  48.2 0.6 %fusion.1 = (bf16[128,128]{1,0:T(8,128)(2,1)}, bf16[128,128]{1,0:T(8,128)(2,1)}) fusion(bf16[128,256]{1,0:T(8,128)(2,1)S(1)} %fusion), kind=kLoop, calls=%fused_computation.5 | loop fusion | bytes 131072 | tf_op jit(solution)/shard_map/slice | solution.py:255
  (4 shorter events, 0.1 us)
Async XLA Ops:
  1.4 16.2 %collective-permute-start = (bf16[128,256]{1,0:T(8,128)(2,1)S(1)}, bf16[128,256]{1,0:T(8,128)(2,1)S(1)}, u32[]{:S(2)}, u32[]{:S(2)}) collective-permute-start(bf16[128,256]{1,0:T(8,128)(2,1)S(1)} %shard_map.84), channel_id=1, source_target_pairs={{0,8},{8,16},{16,24},{24,32},{32,40},{40,48},{48,56},{56,64},{64,7... | collective-permute-start | bytes 196616 | tf_op jit(solution)/shard_map/ppermute | solution.py:36
  17.6 7.5 %collective-permute-start.1 = (bf16[256,256]{1,0:T(8,128)(2,1)S(1)}, bf16[256,256]{1,0:T(8,128)(2,1)S(1)}, u32[]{:S(2)}, u32[]{:S(2)}) collective-permute-start(bf16[256,256]{1,0:T(8,128)(2,1)S(1)} %pad_maximum_fusion.kv_ref.near_ref), channel_id=1, source_target_pairs={{0,32},{8,40},{16,48},{24,56},{32,64},{40,72},{48,80},{56,88},{64,... | collective-permute-start | bytes 393224 | tf_op jit(solution)/shard_map/ppermute | solution.py:36
  19.6 9.9 %collective-permute-start.2 = (bf16[256,256]{1,0:T(8,128)(2,1)S(1)}, bf16[256,256]{1,0:T(8,128)(2,1)S(1)}, u32[]{:S(2)}, u32[]{:S(2)}) collective-permute-start(bf16[256,256]{1,0:T(8,128)(2,1)S(1)} %pad_maximum_fusion.kv_ref.near_ref), channel_id=1, source_target_pairs={{0,16},{8,24},{16,32},{24,40},{32,48},{40,56},{48,64},{56,72},{64,... | collective-permute-start | bytes 393224 | tf_op jit(solution)/shard_map/ppermute | solution.py:36
  31.4 10.0 %collective-permute-start.4 = (bf16[256,256]{1,0:T(8,128)(2,1)S(1)}, bf16[256,256]{1,0:T(8,128)(2,1)S(1)}, u32[]{:S(2)}, u32[]{:S(2)}) collective-permute-start(bf16[256,256]{1,0:T(8,128)(2,1)S(1)} %get-tuple-element.44), channel_id=1, source_target_pairs={{16,0},{24,8},{32,16},{40,24},{48,32},{56,40},{64,48},{72,56},{80,... | collective-permute-start | bytes 393224 | tf_op jit(solution)/shard_map/ppermute | solution.py:36
  35.1 6.2 %collective-permute-start.3 = (bf16[256,256]{1,0:T(8,128)(2,1)S(1)}, bf16[256,256]{1,0:T(8,128)(2,1)S(1)}, u32[]{:S(2)}, u32[]{:S(2)}) collective-permute-start(bf16[256,256]{1,0:T(8,128)(2,1)S(1)} %get-tuple-element.43), channel_id=1, source_target_pairs={{32,0},{40,8},{48,16},{56,24},{64,32},{72,40},{80,48},{88,56},{96,... | collective-permute-start | bytes 393224 | tf_op jit(solution)/shard_map/ppermute | solution.py:36
  41.5 6.7 %collective-permute-start.5 = (bf16[128,256]{1,0:T(8,128)(2,1)S(1)}, bf16[128,256]{1,0:T(8,128)(2,1)S(1)}, u32[]{:S(2)}, u32[]{:S(2)}) collective-permute-start(bf16[128,256]{1,0:T(8,128)(2,1)S(1)} %slice.25), channel_id=1, source_target_pairs={{8,0},{16,8},{24,16},{32,24},{40,32},{48,40},{56,48},{64,56},{72,6... | collective-permute-start | bytes 196616 | tf_op jit(solution)/shard_map/ppermute | solution.py:36

commit v7 on v5

--- a/solution.py
+++ b/solution.py
@@ -17,7 +17,7 @@
 LOG2E = 1.4426950408889634
 NEG = -1e30
 STEP = 2 * TILE
-PIECES = 4
+PIECES = 2
 KEY, VALUE = pl.ds(0, HEAD), pl.ds(HEAD, HEAD)
 
 NT = (((1,), (1,)), ((), ()))

time: 49 us -> 48.9 us (level)
  transfers between devices with their start and end apart: 6 -> 6, of which waited for: 4 -> 4; matrix products, arithmetic and copies ran while one was open for 0% -> 0% of each run, Pallas kernels for 15% -> 14%
where the time goes in v7:
time: 48.9 us; the launch traced here: 48.6 us
  starting transfers between devices  19.3 us (39%)
  waiting for transfers between devices  18.3 us (37%)
  Pallas kernels  9.61 us (20%)
  between operations  0.76 us (2%)
  local copies, waits for them, and re-layouts  0.64 us (1%)
    ppermute x6, starting transfers between devices, shifted(): return lax.ppermute(block, SEQ_AXES, route)  19.3 us
    ppermute x6, waiting for transfers between devices, shifted(): return lax.ppermute(block, SEQ_AXES, route)  18.3 us
    pallas_call x9, Pallas kernels, call(): pl.pallas_call(kernel, out_shape=outs, in_specs=specs, out_specs=(vmem,)...  9.61 us
  transfers between devices with their start and end apart: 6, of which 4 were waited for; matrix products, arithmetic and copies ran while one was open for 0% of the time, Pallas kernels for 14%

profile of v7, /device:TPU:1, one launch (start us, length us, event | category | flops | bytes accessed | tf_op | source)
XLA Modules:
  0.0 48.6 jit_solution(12547679968838542374)
XLA Ops:
  0.6 0.8 %shard_map.84 = bf16[128,256]{1,0:T(8,128)(2,1)S(1)} custom-call(bf16[128,128]{1,0:T(8,128)(2,1)} %k_ref.1, bf16[128,128]{1,0:T(8,128)(2,1)} %v_ref.1), custom_call_target="tpu_custom_call" | custom-call | bytes 131072 | tf_op jit(solution)/shard_map/pallas_call | solution.py:154
  1.4 3.9 %collective-permute-start = (bf16[128,256]{1,0:T(8,128)(2,1)S(1)}, bf16[128,256]{1,0:T(8,128)(2,1)S(1)}, u32[]{:S(2)}, u32[]{:S(2)}) collective-permute-start(bf16[128,256]{1,0:T(8,128)(2,1)S(1)} %shard_map.84), channel_id=1, source_target_pairs={{0,8},{8,16},{16,24},{24,32},{32,40},{40,48},{48,56},{56,64},{64,7... | collective-permute-start | bytes 196616 | tf_op jit(solution)/shard_map/ppermute | solution.py:36
  5.4 12.2 %collective-permute-done = bf16[128,256]{1,0:T(8,128)(2,1)S(1)} collective-permute-done((bf16[128,256]{1,0:T(8,128)(2,1)S(1)}, bf16[128,256]{1,0:T(8,128)(2,1)S(1)}, u32[]{:S(2)}, u32[]{:S(2)}) %collective-permute-start) | collective-permute-done | bytes 65568 | tf_op jit(solution)/shard_map/ppermute | solution.py:36
  17.6 1.9 %collective-permute-start.1 = (bf16[256,256]{1,0:T(8,128)(2,1)S(1)}, bf16[256,256]{1,0:T(8,128)(2,1)S(1)}, u32[]{:S(2)}, u32[]{:S(2)}) collective-permute-start(bf16[256,256]{1,0:T(8,128)(2,1)S(1)} %pad_maximum_fusion.kv_ref.near_ref), channel_id=1, source_target_pairs={{0,32},{8,40},{16,48},{24,56},{32,64},{40,72},{48,80},{56,88},{64,... | collective-permute-start | bytes 393224 | tf_op jit(solution)/shard_map/ppermute | solution.py:36
  19.6 1.9 %collective-permute-start.2 = (bf16[256,256]{1,0:T(8,128)(2,1)S(1)}, bf16[256,256]{1,0:T(8,128)(2,1)S(1)}, u32[]{:S(2)}, u32[]{:S(2)}) collective-permute-start(bf16[256,256]{1,0:T(8,128)(2,1)S(1)} %pad_maximum_fusion.kv_ref.near_ref), channel_id=1, source_target_pairs={{0,16},{8,24},{16,32},{24,40},{32,48},{40,56},{48,64},{56,72},{64,... | collective-permute-start | bytes 393224 | tf_op jit(solution)/shard_map/ppermute | solution.py:36
  21.5 1.2 %shard_map.85 = (bf16[128,2048]{1,0:T(8,128)(2,1)S(1)}, bf16[128,2048]{1,0:T(8,128)(2,1)S(1)}, f32[768,128]{1,0:T(8,128)S(1)}) custom-call(s32[32]{0:T(128)} %lens_hbm.1, s32[1]{0:T(128)} %bitcast.index_ref, bf16[128,2048]{1,0:T(8,128)(2,1)} %q_hbm.1, bf16[128,2048]{1,0:T(8,128)(2,1)} %do_hbm.1), custom_call_target="tpu_custom_call" | custom-call | bytes 2490500 | tf_op jit(solution)/shard_map/pallas_call | solution.py:154
  22.7 1.0 %shard_map.87 = (f32[256,2048]{1,0:T(8,128)S(1)}, f32[256,2048]{1,0:T(8,128)S(1)}, f32[8,2048]{1,0:T(8,128)S(1)}) custom-call(bf16[128,2048]{1,0:T(8,128)(2,1)S(1)} %get-tuple-element.31.qs_ref, bf16[128,2048]{1,0:T(8,128)(2,1)S(1)} %get-tuple-element.32.dos_ref, bf16[256,256]{1,0:T(8,128)(2,1)S(1)} %pad_maximum_fusion.kv_ref.near_ref, ...), custom_call_target="tpu_custom_call" | custom-call | flops 268435456 | bytes 5832704 | tf_op jit(solution)/shard_map/pallas_call | solution.py:154
  23.7 1.4 %collective-permute-done.1.kv_ref.far_ref = bf16[256,256]{1,0:T(8,128)(2,1)S(1)} collective-permute-done((bf16[256,256]{1,0:T(8,128)(2,1)S(1)}, bf16[256,256]{1,0:T(8,128)(2,1)S(1)}, u32[]{:S(2)}, u32[]{:S(2)}) %collective-permute-start.1) | collective-permute-done | bytes 131104 | tf_op jit(solution)/shard_map/ppermute | solution.py:36
  25.1 1.0 %shard_map.86 = (f32[256,2048]{1,0:T(8,128)S(1)}, f32[256,2048]{1,0:T(8,128)S(1)}, f32[8,2048]{1,0:T(8,128)S(1)}) custom-call(bf16[128,2048]{1,0:T(8,128)(2,1)S(1)} %get-tuple-element.31.qs_ref, bf16[128,2048]{1,0:T(8,128)(2,1)S(1)} %get-tuple-element.32.dos_ref, bf16[256,256]{1,0:T(8,128)(2,1)S(1)} %collective-permute-done.1.kv_ref.far_ref, ...), custom_call_target="tpu_custom_call" | custom-call | flops 268435456 | bytes 5832704 | tf_op jit(solution)/shard_map/pallas_call | solution.py:154
  26.1 3.3 %collective-permute-done.2.kv_ref.mid_ref = bf16[256,256]{1,0:T(8,128)(2,1)S(1)} collective-permute-done((bf16[256,256]{1,0:T(8,128)(2,1)S(1)}, bf16[256,256]{1,0:T(8,128)(2,1)S(1)}, u32[]{:S(2)}, u32[]{:S(2)}) %collective-permute-start.2) | collective-permute-done | bytes 131104 | tf_op jit(solution)/shard_map/ppermute | solution.py:36
  29.5 1.0 %shard_map.88 = (f32[256,2048]{1,0:T(8,128)S(1)}, f32[256,2048]{1,0:T(8,128)S(1)}, f32[8,2048]{1,0:T(8,128)S(1)}) custom-call(bf16[128,2048]{1,0:T(8,128)(2,1)S(1)} %get-tuple-element.31.qs_ref, bf16[128,2048]{1,0:T(8,128)(2,1)S(1)} %get-tuple-element.32.dos_ref, bf16[256,256]{1,0:T(8,128)(2,1)S(1)} %collective-permute-done.2.kv_ref.mid_ref, ...), custom_call_target="tpu_custom_call" | custom-call | flops 268435456 | bytes 5963776 | tf_op jit(solution)/shard_map/pallas_call | solution.py:154
  30.5 0.8 %shard_map.90 = (bf16[256,2048]{1,0:T(8,128)(2,1)S(1)}, bf16[256,2048]{1,0:T(8,128)(2,1)S(1)}, bf16[256,256]{1,0:T(8,128)(2,1)S(1)}) custom-call(bf16[128,2048]{1,0:T(8,128)(2,1)S(1)} %get-tuple-element.31.qs_ref, bf16[128,2048]{1,0:T(8,128)(2,1)S(1)} %get-tuple-element.32.dos_ref, f32[256,2048]{1,0:T(8,128)S(1)} %get-tuple-element.40.e_ref, ...), custom_call_target="tpu_custom_call" | custom-call | flops 268435456 | bytes 7536640 | tf_op jit(solution)/shard_map/pallas_call | solution.py:154
  31.4 2.9 %collective-permute-start.4 = (bf16[256,256]{1,0:T(8,128)(2,1)S(1)}, bf16[256,256]{1,0:T(8,128)(2,1)S(1)}, u32[]{:S(2)}, u32[]{:S(2)}) collective-permute-start(bf16[256,256]{1,0:T(8,128)(2,1)S(1)} %get-tuple-element.52), channel_id=1, source_target_pairs={{16,0},{24,8},{32,16},{40,24},{48,32},{56,40},{64,48},{72,56},{80,... | collective-permute-start | bytes 393224 | tf_op jit(solution)/shard_map/ppermute | solution.py:36
  34.3 0.8 %shard_map.89 = (bf16[256,2048]{1,0:T(8,128)(2,1)S(1)}, bf16[256,2048]{1,0:T(8,128)(2,1)S(1)}, bf16[256,256]{1,0:T(8,128)(2,1)S(1)}) custom-call(bf16[128,2048]{1,0:T(8,128)(2,1)S(1)} %get-tuple-element.31.qs_ref, bf16[128,2048]{1,0:T(8,128)(2,1)S(1)} %get-tuple-element.32.dos_ref, f32[256,2048]{1,0:T(8,128)S(1)} %get-tuple-element.34.e_ref, ...), custom_call_target="tpu_custom_call" | custom-call | flops 268435456 | bytes 7536640 | tf_op jit(solution)/shard_map/pallas_call | solution.py:154
  35.1 3.9 %collective-permute-start.3 = (bf16[256,256]{1,0:T(8,128)(2,1)S(1)}, bf16[256,256]{1,0:T(8,128)(2,1)S(1)}, u32[]{:S(2)}, u32[]{:S(2)}) collective-permute-start(bf16[256,256]{1,0:T(8,128)(2,1)S(1)} %get-tuple-element.51), channel_id=1, source_target_pairs={{32,0},{40,8},{48,16},{56,24},{64,32},{72,40},{80,48},{88,56},{96,... | collective-permute-start | bytes 393224 | tf_op jit(solution)/shard_map/ppermute | solution.py:36
  39.1 0.8 %shard_map.91 = (bf16[256,2048]{1,0:T(8,128)(2,1)S(1)}, bf16[256,2048]{1,0:T(8,128)(2,1)S(1)}, f32[256,256]{1,0:T(8,128)S(1)}) custom-call(bf16[128,2048]{1,0:T(8,128)(2,1)S(1)} %get-tuple-element.31.qs_ref, bf16[128,2048]{1,0:T(8,128)(2,1)S(1)} %get-tuple-element.32.dos_ref, f32[256,2048]{1,0:T(8,128)S(1)} %get-tuple-element.43.e_ref, ...), custom_call_target="tpu_custom_call" | custom-call | flops 268435456 | bytes 7667712 | tf_op jit(solution)/shard_map/pallas_call | solution.py:154
  39.9 2.1 %shard_map.92 = (bf16[128,2048]{1,0:T(8,128)(2,1)}, bf16[128,2048]{1,0:T(8,128)(2,1)}) custom-call(bf16[256,256]{1,0:T(8,128)(2,1)S(1)} %collective-permute-done.1.kv_ref.far_ref, bf16[256,256]{1,0:T(8,128)(2,1)S(1)} %collective-permute-done.2.kv_ref.mid_ref, bf16[256,256]{1,0:T(8,128)(2,1)S(1)} %pad_maximum_fusion.kv_ref.near_ref, ...), custom_call_target="tpu_custom_call" | custom-call | flops 805306368 | bytes 7733248 | tf_op jit(solution)/shard_map/pallas_call | solution.py:154
  42.0 0.0 collective-permute-done.4
  42.0 0.0 collective-permute-done.3
  42.0 4.6 %collective-permute-start.5 = (bf16[128,256]{1,0:T(8,128)(2,1)S(1)}, bf16[128,256]{1,0:T(8,128)(2,1)S(1)}, u32[]{:S(2)}, u32[]{:S(2)}) collective-permute-start(bf16[128,256]{1,0:T(8,128)(2,1)S(1)} %slice.25), channel_id=1, source_target_pairs={{8,0},{16,8},{24,16},{32,24},{40,32},{48,40},{56,48},{64,56},{72,6... | collective-permute-start | bytes 196616 | tf_op jit(solution)/shard_map/ppermute | solution.py:36
  46.7 1.3 %collective-permute-done.5 = bf16[128,256]{1,0:T(8,128)(2,1)S(1)} collective-permute-done((bf16[128,256]{1,0:T(8,128)(2,1)S(1)}, bf16[128,256]{1,0:T(8,128)(2,1)S(1)}, u32[]{:S(2)}, u32[]{:S(2)}) %collective-permute-start.5) | collective-permute-done | bytes 65568 | tf_op jit(solution)/shard_map/ppermute | solution.py:36
  48.0 0.6 %fusion.1 = (bf16[128,128]{1,0:T(8,128)(2,1)}, bf16[128,128]{1,0:T(8,128)(2,1)}) fusion(bf16[128,256]{1,0:T(8,128)(2,1)S(1)} %fusion), kind=kLoop, calls=%fused_computation.5 | loop fusion | bytes 131072 | tf_op jit(solution)/shard_map/slice | solution.py:260
  (4 shorter events, 0.1 us)
Async XLA Ops:
  1.4 16.2 %collective-permute-start = (bf16[128,256]{1,0:T(8,128)(2,1)S(1)}, bf16[128,256]{1,0:T(8,128)(2,1)S(1)}, u32[]{:S(2)}, u32[]{:S(2)}) collective-permute-start(bf16[128,256]{1,0:T(8,128)(2,1)S(1)} %shard_map.84), channel_id=1, source_target_pairs={{0,8},{8,16},{16,24},{24,32},{32,40},{40,48},{48,56},{56,64},{64,7... | collective-permute-start | bytes 196616 | tf_op jit(solution)/shard_map/ppermute | solution.py:36
  17.6 7.5 %collective-permute-start.1 = (bf16[256,256]{1,0:T(8,128)(2,1)S(1)}, bf16[256,256]{1,0:T(8,128)(2,1)S(1)}, u32[]{:S(2)}, u32[]{:S(2)}) collective-permute-start(bf16[256,256]{1,0:T(8,128)(2,1)S(1)} %pad_maximum_fusion.kv_ref.near_ref), channel_id=1, source_target_pairs={{0,32},{8,40},{16,48},{24,56},{32,64},{40,72},{48,80},{56,88},{64,... | collective-permute-start | bytes 393224 | tf_op jit(solution)/shard_map/ppermute | solution.py:36
  19.6 9.9 %collective-permute-start.2 = (bf16[256,256]{1,0:T(8,128)(2,1)S(1)}, bf16[256,256]{1,0:T(8,128)(2,1)S(1)}, u32[]{:S(2)}, u32[]{:S(2)}) collective-permute-start(bf16[256,256]{1,0:T(8,128)(2,1)S(1)} %pad_maximum_fusion.kv_ref.near_ref), channel_id=1, source_target_pairs={{0,16},{8,24},{16,32},{24,40},{32,48},{40,56},{48,64},{56,72},{64,... | collective-permute-start | bytes 393224 | tf_op jit(solution)/shard_map/ppermute | solution.py:36
  31.4 10.6 %collective-permute-start.4 = (bf16[256,256]{1,0:T(8,128)(2,1)S(1)}, bf16[256,256]{1,0:T(8,128)(2,1)S(1)}, u32[]{:S(2)}, u32[]{:S(2)}) collective-permute-start(bf16[256,256]{1,0:T(8,128)(2,1)S(1)} %get-tuple-element.52), channel_id=1, source_target_pairs={{16,0},{24,8},{32,16},{40,24},{48,32},{56,40},{64,48},{72,56},{80,... | collective-permute-start | bytes 393224 | tf_op jit(solution)/shard_map/ppermute | solution.py:36
  35.1 6.8 %collective-permute-start.3 = (bf16[256,256]{1,0:T(8,128)(2,1)S(1)}, bf16[256,256]{1,0:T(8,128)(2,1)S(1)}, u32[]{:S(2)}, u32[]{:S(2)}) collective-permute-start(bf16[256,256]{1,0:T(8,128)(2,1)S(1)} %get-tuple-element.51), channel_id=1, source_target_pairs={{32,0},{40,8},{48,16},{56,24},{64,32},{72,40},{80,48},{88,56},{96,... | collective-permute-start | bytes 393224 | tf_op jit(solution)/shard_map/ppermute | solution.py:36
  42.0 5.9 %collective-permute-start.5 = (bf16[128,256]{1,0:T(8,128)(2,1)S(1)}, bf16[128,256]{1,0:T(8,128)(2,1)S(1)}, u32[]{:S(2)}, u32[]{:S(2)}) collective-permute-start(bf16[128,256]{1,0:T(8,128)(2,1)S(1)} %slice.25), channel_id=1, source_target_pairs={{8,0},{16,8},{24,16},{32,24},{40,32},{48,40},{56,48},{64,56},{72,6... | collective-permute-start | bytes 196616 | tf_op jit(solution)/shard_map/ppermute | solution.py:36
